TPU v7x, 256 devices: a whole 4x4x8 slice. The times are simulated.
256 devices in a mesh: seq: 8 (over z_lo, y), outer: 8 (over x, core), inner: 4 (over z_hi).
Axes of the slice: x: 4, y: 4, z: 8 (z_hi: 4, z_lo: 2; z = z_hi * 2 + z_lo), core: 2. Of those that a mesh axis runs over, the one named last changes fastest.
Arguments:
- tokens: bfloat16 [32768, 4096], P(('seq', 'outer', 'inner')), parts along dimension 0, may hold values from -6 to 6
- att_ids: int32 [32768, 2, 2], P(('seq', 'outer', 'inner')), parts along dimension 0, may hold values from 0 to 3, all different within a row
- mlp_ids: int32 [32768, 8], P(('seq', 'outer', 'inner')), parts along dimension 0, may hold values from 0 to 63, all different within a row; in each aligned block of 128 rows (0 to 127, 128 to 255, ...) at most 20 rows name the same one
- att_gain: float32 [4096], replicated, may hold values from 0.25 to 1.75
- att_in: bfloat16 [4096, 768], P('inner'), may hold values from -16 to 16
- att_router: bfloat16 [4096, 8], P('inner'), may hold values from -0.09375 to 0.09375
- att_out: bfloat16 [512, 4096], P(None, 'inner'), may hold values from -0.75 to 0.75
- mlp_gain: float32 [4096], replicated, may hold values from 0.25 to 1.75
- mlp_router: bfloat16 [4096, 64], replicated, may hold values from -0.09375 to 0.09375
- w_up: bfloat16 [64, 4096, 256], P(('outer', 'inner')), may hold values from -0.09375 to 0.09375
- w_down: bfloat16 [64, 256, 4096], P(('outer', 'inner')), may hold values from -0.375 to 0.375
Outputs:
- layer_out: bfloat16 [32768, 4096], P(('seq', 'outer', 'inner')), parts along dimension 0
There are 8 independent parts, one for each index of `seq`. A program takes and returns all parts, laid end to end along the dimension named above; an argument that names none is the same for every part. Nothing has to cross between parts.
Inputs may be any that keep to these rules, and one draw needn't show every extreme that they name: `att_ids`: the 2 ids of one token and head differ. `mlp_ids`: among the rows of one device each expert is named at most 20 times, a bound that some block reaches in some devices' rows.
All inputs are finite; a program needn't handle non-finite values.
Results may differ from a plain program's by a relative error of at most 0.008.
Values may be sent and summed in bfloat16 or wider, within the bound.
A program may use at most 128 MiB of HBM per device.

v0:
```python
import jax
import jax.numpy as jnp
from jax import lax
from jax.sharding import PartitionSpec as P

D = 4096
HEADS = 2
HDIM = 64
ATT_EXP = 4
MLP_TOP = 8


epsilon = 1e-05


def rms_norm(values_in, gain_vector):
    floats = values_in.astype(jnp.float32)
    return (
        floats
        * lax.rsqrt(jnp.mean(floats * floats, axis=-1, keepdims=True) + epsilon)
        * gain_vector
    )


def on_device(
    tokens,
    att_ids,
    mlp_ids,
    att_gain,
    att_in,
    att_router,
    att_out,
    mlp_gain,
    mlp_router,
    w_up,
    w_down,
):
    row_count = tokens.shape[0]
    head_width = HEADS * HDIM
    normed = rms_norm(tokens, att_gain).astype(jnp.bfloat16)
    proj = jnp.dot(
        normed,
        lax.all_gather(att_in, "inner", axis=0, tiled=True),
        preferred_element_type=jnp.float32,
    )
    att_logit = jnp.dot(
        normed,
        lax.all_gather(att_router, "inner", axis=0, tiled=True),
        preferred_element_type=jnp.float32,
    )
    query = proj[:, :head_width].astype(jnp.bfloat16).reshape(row_count, HEADS, HDIM)
    keys = proj[:, head_width : 2 * head_width].astype(jnp.bfloat16)
    value_all = proj[:, 2 * head_width :].reshape(row_count, HEADS, ATT_EXP, HDIM)
    chosen = jnp.sum(
        (att_ids[..., None] == jnp.arange(ATT_EXP)[None, None, None, :]).astype(jnp.float32), axis=2
    )
    att_weight = jax.nn.sigmoid(att_logit.reshape(row_count, HEADS, ATT_EXP)) * chosen
    values = (
        jnp.sum(att_weight[..., None] * value_all, axis=2)
        .astype(jnp.bfloat16)
        .reshape(row_count, head_width)
    )
    first_row = lax.axis_index(("outer", "inner")) * row_count
    query_position = first_row + jnp.arange(row_count)
    score_factor = HDIM ** (-0.5)
    start_state = (
        jnp.full((row_count, HEADS), -1e30, jnp.float32),
        jnp.zeros((row_count, HEADS), jnp.float32),
        jnp.zeros((row_count, HEADS, HDIM), jnp.float32),
    )
    key_piece = lax.all_gather(keys, ("outer", "inner"), axis=0, tiled=True)
    value_piece = lax.all_gather(values, ("outer", "inner"), axis=0, tiled=True)
    piece_rows = key_piece.shape[0]

    def update(current):
        running_max, running_sum, accumulated = current
        key_heads = key_piece.reshape(piece_rows, HEADS, HDIM)
        value_heads = value_piece.reshape(piece_rows, HEADS, HDIM).astype(jnp.float32)
        scores = (
            jnp.einsum("thd,shd->ths", query, key_heads, preferred_element_type=jnp.float32)
            * score_factor
        )
        key_position = jnp.arange(piece_rows)
        visible = key_position[None, None, :] <= query_position[:, None, None]
        scores = jnp.where(visible, scores, -1e30)
        new_max = jnp.maximum(running_max, jnp.max(scores, axis=-1))
        weights = jnp.where(visible, jnp.exp(scores - new_max[..., None]), 0.0)
        new_sum = jnp.sum(weights, axis=-1)
        new_accum = jnp.einsum(
            "ths,shd->thd", weights, value_heads, precision=lax.Precision.HIGHEST
        )
        return (new_max, new_sum, new_accum)

    def keep_state(current):
        return current

    final_state = lax.cond(
        jnp.int32(0) <= first_row + row_count - 1, update, keep_state, start_state
    )
    attended = final_state[2] / final_state[1][..., None]
    head_normed = attended * lax.rsqrt(
        jnp.mean(attended * attended, axis=-1, keepdims=True) + epsilon
    )
    mixed = (head_normed[:, :, None, :] * att_weight[..., None]).reshape(
        row_count, HEADS * ATT_EXP * HDIM
    )
    mixed = mixed.astype(jnp.bfloat16)
    att_result = jnp.dot(
        mixed,
        lax.all_gather(att_out, "inner", axis=1, tiled=True),
        preferred_element_type=jnp.float32,
    )
    hidden_state = tokens.astype(jnp.float32) + att_result
    mlp_in = rms_norm(hidden_state, mlp_gain).astype(jnp.bfloat16)
    logits = jnp.dot(mlp_in, mlp_router, preferred_element_type=jnp.float32)
    expert_total = mlp_router.shape[1]
    picked = (mlp_ids[..., None] == jnp.arange(expert_total)[None, None, :]).astype(jnp.float32)
    gates = jax.nn.sigmoid(jnp.sum(picked * logits[:, None, :], axis=-1))
    outer_count = lax.axis_size("outer")
    inner_count = lax.axis_size("inner")
    device_count = outer_count * inner_count
    local_experts = w_up.shape[0]
    capacity = row_count * MLP_TOP * 5 // (4 * expert_total)
    flat_ids = mlp_ids.reshape(-1)
    one_hot = (flat_ids[:, None] == jnp.arange(expert_total)[None, :]).astype(jnp.int32)
    earlier = jnp.cumsum(one_hot, axis=0) - one_hot
    place_in_expert = jnp.sum(earlier * one_hot, axis=1)
    owner_device = flat_ids // local_experts
    owner_slot = flat_ids % local_experts
    slot_index = (owner_device * capacity + place_in_expert) * local_experts + owner_slot
    token_of_slot = jnp.full((device_count * capacity * local_experts,), row_count, jnp.int32)
    token_of_slot = token_of_slot.at[slot_index].set(jnp.arange(row_count * MLP_TOP) // MLP_TOP)
    padded_rows = jnp.concatenate([mlp_in, jnp.zeros((1, D), jnp.bfloat16)], axis=0)
    outgoing = padded_rows[token_of_slot].reshape(device_count, capacity, local_experts, D)
    hidden = jnp.einsum(
        "scej,ejh->sceh",
        lax.all_to_all(outgoing, ("outer", "inner"), split_axis=0, concat_axis=0, tiled=True),
        w_up,
        preferred_element_type=jnp.float32,
    )
    hidden = jnp.maximum(hidden, 0.0).astype(jnp.bfloat16)
    returned = lax.all_to_all(
        jnp.einsum("sceh,ehj->scej", hidden, w_down, preferred_element_type=jnp.float32).astype(
            jnp.bfloat16
        ),
        ("outer", "inner"),
        split_axis=0,
        concat_axis=0,
        tiled=True,
    )
    result_rows = returned.reshape(-1, D)[slot_index].reshape(row_count, MLP_TOP, D)
    mlp_out = jnp.sum(gates[..., None] * result_rows.astype(jnp.float32), axis=1)
    return (hidden_state + mlp_out).astype(jnp.bfloat16)


def solution(mesh):
    in_specs = (
        P(("seq", "outer", "inner"), None),
        P(("seq", "outer", "inner"), None, None),
        P(("seq", "outer", "inner"), None),
        P(),
        P("inner", None),
        P("inner", None),
        P(None, "inner"),
        P(),
        P(),
        P(("outer", "inner"), None, None),
        P(("outer", "inner"), None, None),
    )
    out_specs = P(("seq", "outer", "inner"), None)
    return jax.shard_map(
        on_device, mesh=mesh, in_specs=in_specs, out_specs=out_specs, check_vma=False
    )
```

profile of v0, /device:TPU:1, one launch (start us, length us, event | category | flops | bytes accessed | tf_op | source)
XLA Modules:
  0.0 934.7 jit_solution(16237632494527740651)
XLA Ops:
  7.3 1.5 fusion.14
  8.9 118.1 %all-gather.5.cloned.1.call-done = bf16[4096,768]{1,0:T(8,128)(2,1)} async-done(((bf16[1024,768]{1,0:T(8,128)(2,1)}), bf16[4096,768]{1,0:T(8,128)(2,1)}) %all-gather.5.cloned.1.call-update) | async-done | bytes 6291472 | tf_op jit(solution)/shard_map/all_gather | solution.py:43
  127.0 4.2 fusion.44
  131.9 17.6 %all_gather.17 = bf16[4096,8]{0,1:T(8,128)(2,1)S(1)} all-gather(bf16[1024,8]{0,1:T(8,128)(2,1)S(1)} %copy-done.8), channel_id=1, replica_groups=mesh['seq'=8,'outer'=8,'inner'=4] {'inner'}, dimensions={0}, use_global_device_ids=true | all-gather | bytes 81920 | tf_op jit(solution)/shard_map/all_gather | solution.py:48
  151.8 18.0 %reduce-window.6 = s32[64,8,128]{2,1,0:T(8,128)S(1)} reduce-window(s32[64,8,128]{2,1,0:T(8,128)S(1)} %fusion.36, s32[]{:T(128)} %constant.87.clone.1), window={size=1x1x128 pad=0_0x0_0x127_0}, to_apply=%region_10.11 | reduce-window | flops 8323072 | bytes 524292 | tf_op jit(solution)/shard_map/reduce-window
  170.5 4.8 scatter_custom_fusion
  175.3 14.7 %all-gather.7.cloned.1.call-done = bf16[4096,128]{1,0:T(8,128)(2,1)} async-done(((bf16[128,128]{1,0:T(8,128)(2,1)}), bf16[4096,128]{1,0:T(8,128)(2,1)}) %all-gather.7.cloned.1.call-update) | async-done | bytes 1048592 | tf_op jit(solution)/shard_map/all_gather | solution.py:71
  190.0 52.0 %all-gather.9.cloned.1.call-done = bf16[4096,128]{0,1:T(8,128)(2,1)} async-done(((bf16[128,128]{0,1:T(8,128)(2,1)}), bf16[4096,128]{0,1:T(8,128)(2,1)}) %all-gather.9.cloned.1.call-update) | async-done | bytes 1048592 | tf_op jit(solution)/shard_map/all_gather | solution.py:72
  242.0 6.6 conditional.1
  245.3 2.5 fusion.7
  248.7 69.2 %all-gather.11.cloned.1.call-done = bf16[512,4096]{1,0:T(8,128)(2,1)} async-done(((bf16[512,1024]{1,0:T(8,128)(2,1)}), bf16[512,4096]{1,0:T(8,128)(2,1)}) %all-gather.11.cloned.1.call-update) | async-done | bytes 4194320 | tf_op jit(solution)/shard_map/all_gather | solution.py:110
  317.9 3.2 multiply_reduce_fusion
  323.8 8.4 gather_fusion
  332.1 17.4 %reshape.252 = bf16[32,20,2,4096]{3,2,1,0:T(2,128)(2,1)} reshape(bf16[1280,4096]{1,0:T(8,128)(2,1)} %gather_fusion) | data formatting | bytes 20971520 | tf_op jit(solution)/shard_map/reshape | solution.py:134
  349.5 246.8 %all_to_all.10 = bf16[32,20,2,4096]{3,2,1,0:T(2,128)(2,1)S(1)} all-to-all(bf16[32,20,2,4096]{3,2,1,0:T(2,128)(2,1)} %reshape.252), channel_id=1, replica_groups=mesh['seq'=8,'outer'=8,'inner'=4] {'outer','inner'}, dimensions={0} | all-to-all | bytes 20971520 | tf_op jit(solution)/shard_map/all_to_all | solution.py:137
  596.3 11.1 %fusion.21 = bf16[32,20,2,256]{3,1,0,2:T(8,128)(2,1)} fusion(bf16[2,4096,256]{2,1,0:T(8,128)(2,1)} %param.22, bf16[32,20,2,4096]{3,2,1,0:T(2,128)(2,1)S(1)} %all_to_all.10), kind=kOutput, calls=%fused_computation.34 | convolution fusion | flops 2685009920 | bytes 15335424 | tf_op jit(solution)/shard_map/scej,ejh->sceh/dot_general | solution.py:135
  607.4 5.3 convert_bitcast_fusion
  612.7 25.4 %copy.112 = bf16[32,20,2,4096]{3,2,1,0:T(2,128)(2,1)} copy(bf16[32,20,2,4096]{3,0,1,2:T(8,128)(2,1)S(1)} %convert_bitcast_fusion) | data formatting | bytes 20971520 | tf_op jit(solution)/shard_map/convert_element_type | solution.py:143
  638.1 7.4 all-to-all-start.1
  646.2 229.2 %all-to-all-done.1 = bf16[32,20,2,4096]{3,2,1,0:T(2,128)(2,1)} async-done(((bf16[32,20,2,4096]{3,2,1,0:T(2,128)(2,1)}), bf16[32,20,2,4096]{3,2,1,0:T(2,128)(2,1)}, u32[]{:S(2)}, u32[]{:S(2)}) %all-to-all-start.1) | async-done | bytes 10485792 | tf_op jit(solution)/shard_map/all_to_all | solution.py:142
  875.4 16.0 %reshape.253 = bf16[1280,4096]{1,0:T(8,128)(2,1)} reshape(bf16[32,20,2,4096]{3,2,1,0:T(2,128)(2,1)} %all-to-all-done.1) | data formatting | bytes 20971520 | tf_op jit(solution)/shard_map/reshape | solution.py:151
  891.5 20.4 %gather_fusion.1 = bf16[1024,4096]{1,0:T(8,128)(2,1)} fusion(bf16[1280,4096]{1,0:T(8,128)(2,1)} %reshape.253, s32[1024]{0:T(1024)S(1)} %broadcast_clamp_fusion), kind=kCustom, calls=%fused_computation.1 | custom fusion | bytes 16781312 | tf_op jit(solution)/shard_map/gather | solution.py:151
  911.9 13.3 %fusion.9 = f32[128,4096]{1,0:T(8,128)} fusion(bf16[1024,4096]{1,0:T(8,128)(2,1)} %gather_fusion.1, f32[128,8]{1,0:T(8,128)S(1)} %copy.104), kind=kLoop, calls=%fused_computation.18 | loop fusion | flops 12058624 | bytes 10489856 | tf_op jit(solution)/shard_map/reduce_sum | solution.py:152
  925.2 2.8 add_convert_fusion
  (77 shorter events, 11.8 us)
Async XLA Ops:
  6.5 639.0 %copy-start = (bf16[4096,64]{0,1:T(8,128)(2,1)S(1)}, bf16[4096,64]{0,1:T(8,128)(2,1)}, u32[]{:S(2)}) copy-start(bf16[4096,64]{0,1:T(8,128)(2,1)} %param.21) | copy-start | bytes 1572868
  6.5 120.5 %all-gather.5.cloned.1.call-start = ((), (), s32[]{:S(2)}) async-start(), calls=%async_computation.2 | async-start | bytes 7864320 | tf_op jit(solution)/shard_map/all_gather | solution.py:43
  7.3 182.7 %all-gather.7.cloned.1.call-start = ((), (), s32[]{:S(2)}) async-start(), calls=%async_computation.3 | async-start | bytes 1081344 | tf_op jit(solution)/shard_map/all_gather | solution.py:71
  8.8 123.1 %copy-start.8 = (bf16[1024,8]{0,1:T(8,128)(2,1)S(1)}, bf16[1024,8]{0,1:T(8,128)(2,1)}, u32[]{:S(2)}) copy-start(bf16[1024,8]{0,1:T(8,128)(2,1)} %param.18) | copy-start | bytes 49156
  8.8 140.7 %copy-start.10 = (s32[128,2,2]{0,2,1:T(2,128)S(1)}, s32[128,2,2]{0,2,1:T(2,128)}, u32[]{:S(2)}) copy-start(s32[128,2,2]{0,2,1:T(2,128)} %param.14) | copy-start | bytes 6148
  8.8 140.7 %copy-start.3 = (bf16[128,4096]{1,0:T(8,128)(2,1)S(1)}, bf16[128,4096]{1,0:T(8,128)(2,1)}, u32[]{:S(2)}) copy-start(bf16[128,4096]{1,0:T(8,128)(2,1)} %param.13) | copy-start | bytes 3145732
  8.9 140.7 %copy-start.6 = (f32[4096]{0:T(1024)S(1)}, f32[4096]{0:T(1024)}, u32[]{:S(2)}) copy-start(f32[4096]{0:T(1024)} %param.16) | copy-start | bytes 49156
  131.2 20.2 %copy-start.9 = (s32[128,8]{0,1:T(8,128)S(1)}, s32[128,8]{0,1:T(8,128)}, u32[]{:S(2)}) copy-start(s32[128,8]{0,1:T(8,128)} %param.15) | copy-start | bytes 12292
  131.8 110.2 %all-gather.9.cloned.1.call-start = ((), (), s32[]{:S(2)}) async-start(), calls=%async_computation.4 | async-start | bytes 1081344 | tf_op jit(solution)/shard_map/all_gather | solution.py:72
  150.8 167.1 %all-gather.11.cloned.1.call-start = ((), (), s32[]{:S(2)}) async-start(), calls=%async_computation.5 | async-start | bytes 5242880 | tf_op jit(solution)/shard_map/all_gather | solution.py:110
  244.1 1.2 copy-start.11
  317.9 4.5 copy-start.7
  321.0 1.3 copy-start.1
  322.7 1.0 copy-start.4
  638.1 7.5 copy-start.5
  638.1 237.3 %all-to-all-start.1 = ((bf16[32,20,2,4096]{3,2,1,0:T(2,128)(2,1)}), bf16[32,20,2,4096]{3,2,1,0:T(2,128)(2,1)}, u32[]{:S(2)}, u32[]{:S(2)}) async-start(bf16[32,20,2,4096]{3,2,1,0:T(2,128)(2,1)} %copy.112), calls=%async_computation.1 | async-start | bytes 20971520 | tf_op jit(solution)/shard_map/all_to_all | solution.py:142
  911.9 13.3 %copy-start.2 = (f32[128,4096]{1,0:T(8,128)S(1)}, f32[128,4096]{1,0:T(8,128)}, u32[]{:S(2)}) copy-start(f32[128,4096]{1,0:T(8,128)} %copy-done.1) | copy-start | bytes 6291460
Sparse Core Ops, SparseCore 0:
  9.2 117.7 all-gather.4
  131.9 57.9 all-gather.6
  192.5 49.5 all-gather.8
  243.7 74.1 all-gather.10
where the time goes:
time: 942 us; the launch traced here: 935 us
  waiting for transfers between devices  484 us (51%)
  blocking collectives  264 us (28%)
  local copies, waits for them, and re-layouts  98.1 us (10%)
  other arithmetic  38.2 us (4%)
  matrix products  28.3 us (3%)
  between operations  13.7 us (1%)
    all_to_all x1, blocking collectives, on_device(): lax.all_to_all(outgoing, ('outer', 'inner'), split_axis=0, concat_axis=0,...  247 us
    all_to_all x1, waiting for transfers between devices, on_device(): lax.all_to_all(jnp.einsum('sceh,ehj->scej', hidden, w_down, preferred_ele...  229 us
    all_gather x1, waiting for transfers between devices, on_device(): lax.all_gather(att_in, 'inner', axis=0, tiled=True)  118 us
    all_gather x1, waiting for transfers between devices, on_device(): lax.all_gather(att_out, 'inner', axis=1, tiled=True)  69.2 us
    all_gather x1, waiting for transfers between devices, on_device(): value_piece = lax.all_gather(values, ('outer', 'inner'), axis=0, tiled=True)  52 us
    convert_element_type x1, local copies, waits for them, and re-layouts, on_device(): jnp.einsum('sceh,ehj->scej', hidden, w_down, preferred_element_type=jnp.f...  25.4 us
    gather x1, local copies, waits for them, and re-layouts, on_device(): returned.reshape(-1, D)[slot_index].reshape(row_count, MLP_TOP, D)  20.4 us
  transfers between devices with their start and end apart: 5, of which 5 were waited for; matrix products, arithmetic and copies ran while one was open for 4% of the time, Pallas kernels for 0%

commit v1 on v0

v1 whole, which is shorter than its diff:
```python
import functools

import jax
import jax.numpy as jnp
from jax import lax
from jax.experimental import pallas as pl
from jax.experimental.pallas import tpu as pltpu
from jax.sharding import PartitionSpec as P

D = 4096
HEADS = 2
HDIM = 64
ATT_EXP = 4
EXT = D + 128
ROWS = 128
epsilon = 1e-05
MESH = pl.DeviceIdType.MESH
ANY = pl.BlockSpec(memory_space=pl.ANY)
VM = pl.BlockSpec(memory_space=pltpu.VMEM)
DMA = pltpu.SemaphoreType.DMA
BF = jnp.bfloat16
F32 = jnp.float32


def rms_norm(values_in, gain_vector):
    floats = values_in.astype(F32)
    return (
        floats
        * lax.rsqrt(jnp.mean(floats * floats, axis=-1, keepdims=True) + epsilon)
        * gain_vector
    )


class Place:
    def __init__(self):
        self.seq, self.outer, self.inner = (lax.axis_index(a) for a in ("seq", "outer", "inner"))
        self.zl, self.y = self.seq // 4, self.seq % 4
        self.x, self.c = self.outer // 2, self.outer % 2

    def along_z(self, d):
        return (self.seq, self.outer, (self.inner + d) % 4)

    def along_y(self, d):
        return (self.zl * 4 + (self.y + d) % 4, self.outer, self.inner)

    def along_x(self, d):
        return (self.seq, ((self.x + d) % 4) * 2 + self.c, self.inner)

    def sibling(self):
        return (self.seq, self.x * 2 + 1 - self.c, self.inner)

    def pair(self):
        return ((1 - self.zl) * 4 + self.y, self.outer, self.inner)

    def beyond(self):
        return ((1 - self.zl) * 4 + self.y, self.outer, (self.inner + 2 * self.zl - 1) % 4)


def meet(peers):
    barrier = pltpu.get_barrier_semaphore()
    for peer in peers:
        pl.semaphore_signal(barrier, inc=1, device_id=peer, device_id_type=MESH)
    pl.semaphore_wait(barrier, len(peers))


def remote(src, dst, send, recv, peer):
    return pltpu.make_async_remote_copy(
        src_ref=src, dst_ref=dst, send_sem=send, recv_sem=recv, device_id=peer, device_id_type=MESH
    )


def spread_over_z(at, own, gathered, full, p, sems):
    s1, r1, s2, r2, s3, r3 = sems
    n = full // 16
    spans = (
        pl.ds(pl.multiple_of(p.c * (4 * n) + p.y * n, n), n),
        pl.ds(pl.multiple_of(8 * n + p.c * (4 * n) + p.x * n, n), n),
    )
    halves = tuple(pl.ds(pl.multiple_of(8 * n * h + p.c * (4 * n), 4 * n), 4 * n) for h in range(2))

    def first(d, h):
        return remote(
            own.at[spans[h]], gathered.at[p.inner, spans[h]], s1.at[at, d - 1, h], r1.at[at, d - 1, h], p.along_z(d)
        )

    def second(d, h, e):
        j = (p.inner - d + 4) % 4
        peer = p.along_y(e) if h == 0 else p.along_x(e)
        block = gathered.at[j, spans[h]]
        return remote(block, block, s2.at[at, d - 1, h, e - 1], r2.at[at, d - 1, h, e - 1], peer)

    def third(d, h):
        j = (p.inner - d + 4) % 4
        block = gathered.at[j, halves[h]]
        return remote(block, block, s3.at[at, d - 1, h], r3.at[at, d - 1, h], p.sibling())

    order = (1, 3, 2)
    every = [(d, h) for d in order for h in range(2)]

    def go1():
        for d, h in every:
            first(d, h).start()

    def go2(d):
        for h in range(2):
            first(d, h).wait_recv()
            for e in (1, 3, 2):
                second(d, h, e).start()

    def go3(d):
        for h in range(2):
            for e in (1, 3, 2):
                second(d, h, e).wait_recv()
            third(d, h).start()

    def end():
        for d, h in every:
            third(d, h).wait_recv()
        for d, h in every:
            first(d, h).wait_send()
            third(d, h).wait_send()
            for e in (1, 3, 2):
                second(d, h, e).wait_send()

    return order, go1, go2, go3, end


def spread_sems(n):
    return [DMA((n, 3, 2)), DMA((n, 3, 2)), DMA((n, 3, 2, 3)), DMA((n, 3, 2, 3)), DMA((n, 3, 2)), DMA((n, 3, 2))]


def square_peers(p):
    return (
        [p.along_z(d) for d in (1, 2, 3)]
        + [p.along_y(d) for d in (1, 2, 3)]
        + [p.along_x(d) for d in (1, 2, 3)]
        + [p.sibling()]
    )


def att_in_kernel(w, r, gw, gr, s1, r1, s2, r2, s3, r3, sr, rr, local):
    p = Place()
    copies = [
        pltpu.make_async_copy(w, gw.at[p.inner], local.at[0]),
        pltpu.make_async_copy(r, gr.at[p.inner], local.at[1]),
    ]
    for copy in copies:
        copy.start()
    meet(square_peers(p))
    order, go1, go2, go3, end = spread_over_z(0, w, gw, 1024, p, (s1, r1, s2, r2, s3, r3))
    go1()
    routers = [remote(r, gr.at[p.inner], sr.at[d - 1], rr.at[d - 1], p.along_z(d)) for d in (1, 2, 3)]
    for copy in routers:
        copy.start()
    for d in order:
        go2(d)
    for d in order:
        go3(d)
    end()
    for copy in routers:
        copy.wait()
    for copy in copies:
        copy.wait()


def gather_att_in(att_in, router_t):
    return pl.pallas_call(
        att_in_kernel,
        out_shape=(
            jax.ShapeDtypeStruct((4, 1024, 768), BF),
            jax.ShapeDtypeStruct((4, 8, 1024), BF),
        ),
        in_specs=[ANY, ANY],
        out_specs=(ANY, ANY),
        scratch_shapes=spread_sems(1) + [DMA((3,)), DMA((3,)), DMA((2,))],
        compiler_params=pltpu.CompilerParams(collective_id=1, has_side_effects=True, vmem_limit_bytes=2**20),
        name="gather_att_in",
    )(att_in, router_t)


def kv_kernel(kv, w, gk, gw, s1, r1, s2, r2, s3, r3, sz, rz, sx, rx, sc, rc, local):
    p = Place()
    copies = [
        pltpu.make_async_copy(w, gw.at[p.inner], local.at[0]),
        pltpu.make_async_copy(kv, gk.at[p.outer, p.inner], local.at[1]),
    ]
    for copy in copies:
        copy.start()
    meet(square_peers(p))
    order, go1, go2, go3, end = spread_over_z(0, w, gw, 512, p, (s1, r1, s2, r2, s3, r3))
    zs = [remote(kv, gk.at[p.outer, p.inner], sz.at[d - 1], rz.at[d - 1], p.along_z(d)) for d in (1, 2, 3)]
    xs = [
        remote(gk.at[p.outer], gk.at[p.outer], sx.at[d - 1], rx.at[d - 1], p.along_x(d)) for d in (1, 2, 3)
    ]
    cs = []
    for d in range(4):
        o = ((p.x - d + 4) % 4) * 2 + p.c
        cs.append(remote(gk.at[o], gk.at[o], sc.at[d], rc.at[d], p.sibling()))
    for copy in zs:
        copy.start()
    go1()
    copies[1].wait()
    for copy in zs:
        copy.wait_recv()
    for copy in (xs[0], xs[2], xs[1]):
        copy.start()
    cs[0].start()
    for d in order:
        go2(d)
    for d in (1, 3, 2):
        xs[d - 1].wait_recv()
        cs[d].start()
    for d in order:
        go3(d)
    end()
    for copy in cs:
        copy.wait()
    for copy in zs + xs:
        copy.wait_send()
    copies[0].wait()


def gather_kv(kv, att_out):
    return pl.pallas_call(
        kv_kernel,
        out_shape=(
            jax.ShapeDtypeStruct((8, 4, ROWS, 256), BF),
            jax.ShapeDtypeStruct((4, 512, 1024), BF),
        ),
        in_specs=[ANY, ANY],
        out_specs=(ANY, ANY),
        scratch_shapes=spread_sems(1)
        + [DMA((3,)), DMA((3,)), DMA((3,)), DMA((3,)), DMA((4,)), DMA((4,)), DMA((2,))],
        compiler_params=pltpu.CompilerParams(collective_id=2, has_side_effects=True, vmem_limit_bytes=2**20),
        name="gather_kv",
    )(kv, att_out)


class Weights:
    def __init__(self, p, own, gathered, sems):
        self.p, self.own, self.gathered = p, own, gathered
        self.ns, self.fr, self.ps, self.sr, self.ys, self.yr = sems
        self.k = p.y % 2
        self.step = 2 * p.zl - 1

    def part(self, ref, kind, e, c):
        span = pl.ds(pl.multiple_of(c * 512, 512), 512)
        return ref.at[e, span, :] if kind == 0 else ref.at[e, :, span]

    def chunk(self, kind, shard, c):
        return self.part(self.gathered[kind], kind, ((shard + 8) % 4) * 2 + self.k, c)

    def to_next(self, kind, m, t):
        p = self.p
        if t < 2:
            src = self.part(self.own[kind], kind, self.k, 2 * m + t)
            dst = self.chunk(kind, p.inner, 2 * m + t)
        else:
            src = dst = self.chunk(kind, p.inner - self.step, 2 * m + 1 - p.zl)
        return remote(src, dst, self.ns.at[kind, m, t], self.fr.at[kind, m, t], p.beyond())

    def far(self, kind, m, t):
        p = self.p
        return (p.inner + self.step, 2 * m + t) if t < 2 else (p.inner + 2, 2 * m + p.zl)

    def near(self, kind, m, t):
        p = self.p
        return (p.inner - self.step, 2 * m + t) if t < 2 else (p.inner + 2, 2 * m + 1 - p.zl)

    def forward(self, kind, m, t):
        block = self.chunk(kind, *self.far(kind, m, t))
        return remote(block, block, self.ps.at[kind, m, t], self.sr.at[kind, m, t], self.p.pair())

    def sideways(self, kind, m, t, which):
        shard, c = (self.far, self.near)[which](kind, m, t)
        block = self.chunk(kind, shard, c)
        peer = self.p.along_y(5 - 2 * (c % 2))
        return remote(block, block, self.ys.at[kind, m, t, which], self.yr.at[kind, m, t, which], peer)

    def begin(self, kind, m):
        for t in range(2):
            self.to_next(kind, m, t).start()

    def turn(self, kind, m, after=None):
        if after is not None:
            self.begin(*after)
        for t in range(3):
            self.to_next(kind, m, t).wait_recv()
            self.forward(kind, m, t).start()
            self.sideways(kind, m, t, 0).start()
            self.forward(kind, m, t).wait_recv()
            self.sideways(kind, m, t, 1).start()
            if t == 1:
                self.to_next(kind, m, 2).start()

    def settle(self, kind, m):
        for t in range(3):
            for which in range(2):
                self.sideways(kind, m, t, which).wait_recv()

    def drain(self, kind, m):
        for t in range(3):
            self.to_next(kind, m, t).wait_send()
            self.forward(kind, m, t).wait_send()
            for which in range(2):
                self.sideways(kind, m, t, which).wait_send()

    def peers(self):
        p = self.p
        return [p.beyond(), p.pair(), p.along_y(1), p.along_y(3)]


def weight_sems():
    return [DMA((2, 4, 3))] * 4 + [DMA((2, 4, 3, 2))] * 2


def moe_kernel(
    ext, hs, up, down, out, gup, gdn,
    xall, acc, hid, wbuf, dbuf, part, pairbuf, xbuf,
    ns, fr, ps, sr, ys, yr, ts, tr, us, ur, vs, vr, es, er, qs, qr, local, load,
):
    p = Place()
    w = Weights(p, (up, down), (gup, gdn), (ns, fr, ps, sr, ys, yr))
    own_copies = [
        pltpu.make_async_copy(up, gup.at[pl.ds(2 * p.inner, 2)], local.at[0]),
        pltpu.make_async_copy(down, gdn.at[pl.ds(2 * p.inner, 2)], local.at[1]),
    ]
    for copy in own_copies:
        copy.start()
    meet(w.peers() + [p.along_x(1), p.along_x(2), p.along_x(3), p.sibling()])
    w.begin(0, 0)

    def rows(o, h):
        return xall.at[o, pl.ds(64 * h, 64), :]

    def block(d):
        return ((p.x + d) % 4) * 2 + p.c

    def mine(d, h):
        src = ext.at[pl.ds(64 * h, 64), :]
        return remote(src, rows(p.outer, h), ts.at[(d - 1) // 2, h], tr.at[(d - 1) // 2, h], p.along_x(d))

    def relay(d):
        h = (d - 1) // 2
        src = rows(block(4 - d), h)
        return remote(src, src, us.at[h], ur.at[h], p.along_x(d))

    def across(d, h):
        src = ext.at[pl.ds(64 * h, 64), :] if d == 0 else rows(block(d), h)
        return remote(src, rows(block(d), h), vs.at[d, h], vr.at[d, h], p.sibling())

    for h in range(2):
        for d in (1, 3):
            mine(d, h if d == 1 else 1 - h).start()
    for h in range(2):
        across(0, h).start()
    keep = pltpu.make_async_copy(ext, xall.at[p.outer], local.at[2])
    keep.start()

    w.turn(0, 0, (0, 1))
    mine(1, 0).wait_recv()
    relay(1).start()
    across(3, 0).start()
    mine(3, 1).wait_recv()
    relay(3).start()
    across(1, 1).start()
    mine(1, 1).wait_recv()
    across(3, 1).start()
    mine(3, 0).wait_recv()
    across(1, 0).start()
    w.turn(0, 1, (0, 2))
    for d in (1, 3):
        relay(d).wait_recv()
        across(2, (d - 1) // 2).start()
    for copy in own_copies:
        copy.wait()

    def load_up(m):
        return pltpu.make_async_copy(
            gup.at[:, pl.ds(1024 * m, 1024), :], wbuf.at[m % 2], load.at[m % 2]
        )

    def load_down(m):
        return pltpu.make_async_copy(
            gdn.at[:, :, pl.ds(1024 * m, 1024)], dbuf.at[m % 2], load.at[m % 2]
        )

    def run_up(m):
        xs = xall.at[:, :, pl.ds(1024 * m, 1024)]

        def one(e, carry):
            got = jnp.dot(
                xs[...].reshape(1024, 1024), wbuf[m % 2, e], preferred_element_type=F32
            )
            if m == 0:
                acc[e] = got
            else:
                acc[e] += got
            return carry

        lax.fori_loop(0, 8, one, 0)

    def gate():
        names = lax.broadcasted_iota(jnp.int32, (128, 256), 0) % 64
        shares = xall[:, :, D:].reshape(1024, 128)

        def one(e, carry):
            pick = jnp.where(names == p.outer * 8 + e, 1.0, 0.0).astype(BF)
            scale = jnp.dot(shares, pick, preferred_element_type=F32)
            hid[:, pl.ds(pl.multiple_of(256 * e, 256), 256)] = (jnp.maximum(acc[e], 0.0) * scale).astype(BF)
            return carry

        lax.fori_loop(0, 8, one, 0)

    def run_down(m):
        def one(n, carry):
            span = pl.ds(pl.multiple_of(256 * n, 256), 256)
            weights = dbuf[m % 2, :, :, span].reshape(2048, 256)
            got = jnp.dot(hid[...], weights, preferred_element_type=F32)
            part[m, :, :, :, span] = got.astype(BF).reshape(4, 2, 128, 256)
            return carry

        lax.fori_loop(0, 4, one, 0)

    def swap(m):
        return remote(part.at[m, :, 1 - p.c], pairbuf.at[m], es.at[m], er.at[m], p.sibling())

    def give(m, d):
        there = (p.x + d) % 4
        return remote(part.at[m, there, p.c], xbuf.at[m, d - 1], qs.at[m, d - 1], qr.at[m, d - 1], p.along_x(d))

    def add_pair(m):
        swap(m).wait_recv()
        for d in (1, 3, 2):
            there = (p.x + d) % 4
            total = part[m, there, p.c].astype(F32) + pairbuf[m, there].astype(F32)
            part[m, there, p.c] = total.astype(BF)
            give(m, d).start()

    def finish(m):
        span = pl.ds(1024 * m, 1024)
        total = hs[:, span] + part[m, p.x, p.c].astype(F32) + pairbuf[m, p.x].astype(F32)
        for d in (1, 3, 2):
            give(m, d).wait_recv()
            total += xbuf[m, d - 1].astype(F32)
        out[:, span] = total.astype(BF)

    w.settle(0, 0)
    load_up(0).start()
    w.turn(0, 2, (0, 3))
    keep.wait()
    for d in range(4):
        for h in range(2):
            across(d, h).wait_recv()
    w.settle(0, 1)
    load_up(1).start()
    load_up(0).wait()
    run_up(0)
    w.turn(0, 3, (1, 0))
    w.settle(0, 2)
    load_up(2).start()
    load_up(1).wait()
    run_up(1)
    w.turn(1, 0, (1, 1))
    w.settle(0, 3)
    load_up(3).start()
    load_up(2).wait()
    run_up(2)
    w.settle(1, 0)
    load_down(0).start()
    load_up(3).wait()
    run_up(3)
    gate()
    w.turn(1, 1, (1, 2))
    w.settle(1, 1)
    load_down(1).start()
    load_down(0).wait()
    run_down(0)
    swap(0).start()
    w.turn(1, 2, (1, 3))
    w.settle(1, 2)
    load_down(2).start()
    load_down(1).wait()
    run_down(1)
    swap(1).start()
    add_pair(0)
    w.turn(1, 3)
    load_down(2).wait()
    run_down(2)
    swap(2).start()
    add_pair(1)
    finish(0)
    w.settle(1, 3)
    load_down(3).start()
    load_down(3).wait()
    run_down(3)
    swap(3).start()
    add_pair(2)
    add_pair(3)
    for m in (1, 2, 3):
        finish(m)
    for kind in range(2):
        for m in range(4):
            w.drain(kind, m)
    for h in range(2):
        for d in (1, 3):
            mine(d, h).wait_send()
        for d in range(4):
            across(d, h).wait_send()
    for d in (1, 3):
        relay(d).wait_send()
    for m in range(4):
        swap(m).wait_send()
        for d in (1, 2, 3):
            give(m, d).wait_send()


def moe(ext, hidden_state, w_up, w_down):
    return pl.pallas_call(
        moe_kernel,
        out_shape=(
            jax.ShapeDtypeStruct((ROWS, D), BF),
            jax.ShapeDtypeStruct((8, D, 256), BF),
            jax.ShapeDtypeStruct((8, 256, D), BF),
        ),
        in_specs=[VM, VM, ANY, ANY],
        out_specs=(VM, ANY, ANY),
        scratch_shapes=[
            pltpu.VMEM((8, ROWS, EXT), BF),
            pltpu.VMEM((8, 1024, 256), F32),
            pltpu.VMEM((1024, 2048), BF),
            pltpu.VMEM((2, 8, 1024, 256), BF),
            pltpu.VMEM((2, 8, 256, 1024), BF),
            pltpu.VMEM((4, 4, 2, ROWS, 1024), BF),
            pltpu.VMEM((4, 4, ROWS, 1024), BF),
            pltpu.VMEM((4, 3, ROWS, 1024), BF),
        ]
        + weight_sems()
        + [
            DMA((2, 2)), DMA((2, 2)), DMA((2,)), DMA((2,)), DMA((4, 2)), DMA((4, 2)),
            DMA((4,)), DMA((4,)), DMA((4, 3)), DMA((4, 3)), DMA((3,)), DMA((2,)),
        ],
        compiler_params=pltpu.CompilerParams(collective_id=3, has_side_effects=True, vmem_limit_bytes=60 * 2**20),
        name="experts",
    )(ext, hidden_state, w_up, w_down)[0]


def on_device(
    tokens,
    att_ids,
    mlp_ids,
    att_gain,
    att_in,
    att_router,
    att_out,
    mlp_gain,
    mlp_router,
    w_up,
    w_down,
):
    row_count = tokens.shape[0]
    head_width = HEADS * HDIM
    in_all, router_all = gather_att_in(att_in, att_router.T)
    normed = rms_norm(tokens, att_gain).astype(BF)
    proj = jnp.dot(normed, in_all.reshape(D, 768), preferred_element_type=F32)
    att_logit = jnp.einsum(
        "tsk,snk->tn", normed.reshape(row_count, 4, 1024), router_all, preferred_element_type=F32
    )
    query = proj[:, :head_width].astype(BF).reshape(row_count, HEADS, HDIM)
    keys = proj[:, head_width : 2 * head_width].astype(BF)
    value_all = proj[:, 2 * head_width :].reshape(row_count, HEADS, ATT_EXP, HDIM)
    chosen = jnp.sum(
        (att_ids[..., None] == jnp.arange(ATT_EXP)[None, None, None, :]).astype(F32), axis=2
    )
    att_weight = jax.nn.sigmoid(att_logit.reshape(row_count, HEADS, ATT_EXP)) * chosen
    values = jnp.sum(att_weight[..., None] * value_all, axis=2).astype(BF).reshape(row_count, head_width)
    kv_all, out_all = gather_kv(jnp.concatenate([keys, values], axis=1), att_out)
    kv_rows = kv_all.reshape(-1, 4, HDIM)
    first_row = lax.axis_index(("outer", "inner")) * row_count
    query_position = first_row + jnp.arange(row_count)
    scores = jnp.einsum("thd,shd->hts", query, kv_rows[:, :HEADS], preferred_element_type=F32) * HDIM ** (-0.5)
    visible = jnp.arange(kv_rows.shape[0])[None, None, :] <= query_position[None, :, None]
    scores = jnp.where(visible, scores, -1e30)
    weights = jnp.exp(scores - jnp.max(scores, axis=-1, keepdims=True))
    total = jnp.sum(weights, axis=-1)
    attended = jnp.einsum("hts,shd->thd", weights.astype(BF), kv_rows[:, HEADS:], preferred_element_type=F32)
    attended = attended / total.T[..., None]
    head_normed = attended * lax.rsqrt(jnp.mean(attended * attended, axis=-1, keepdims=True) + epsilon)
    mixed = (head_normed[:, :, None, :] * att_weight[..., None]).reshape(row_count, HEADS * ATT_EXP * HDIM)
    mixed = mixed.astype(BF)
    att_result = jnp.einsum("tk,skn->tsn", mixed, out_all, preferred_element_type=F32).reshape(row_count, D)
    hidden_state = tokens.astype(F32) + att_result
    mlp_in = rms_norm(hidden_state, mlp_gain).astype(BF)
    logits = jnp.dot(mlp_in, mlp_router, preferred_element_type=F32)
    picked = jnp.any(mlp_ids[..., None] == jnp.arange(mlp_router.shape[1])[None, None, :], axis=1)
    gates = jnp.where(picked, jax.nn.sigmoid(logits), 0.0)
    high = lax.reduce_precision(gates, 8, 7)
    ext = jnp.concatenate([mlp_in, high.astype(BF), (gates - high).astype(BF)], axis=1)
    return moe(ext, hidden_state, w_up, w_down)


def solution(mesh):
    in_specs = (
        P(("seq", "outer", "inner"), None),
        P(("seq", "outer", "inner"), None, None),
        P(("seq", "outer", "inner"), None),
        P(),
        P("inner", None),
        P("inner", None),
        P(None, "inner"),
        P(),
        P(),
        P(("outer", "inner"), None, None),
        P(("outer", "inner"), None, None),
    )
    out_specs = P(("seq", "outer", "inner"), None)
    return jax.shard_map(
        on_device, mesh=mesh, in_specs=in_specs, out_specs=out_specs, check_vma=False
    )
```

time: 942 us -> 622 us (0.66)
  Pallas kernels: 0 us -> 580 us
  waiting for transfers between devices: 484 us -> 0 us
  blocking collectives: 264 us -> 0 us
  local copies, waits for them, and re-layouts: 98.1 us -> 22.6 us
  other arithmetic: 38.2 us -> 6.43 us
  matrix products: 28.3 us -> 6.74 us
  between operations: 13.7 us -> 0.3 us
    pallas_call x0 -> x3, Pallas kernels: none -> 580 us  [the longest x1 508 us: moe(): pl.pallas_call(moe_kernel, out_shape=(jax.ShapeDtypeStruct((ROWS, D), BF)...]
    all_gather x4 -> x0, waiting for transfers between devices: 254 us -> none  [the longest x1 118 us: on_device(): lax.all_gather(att_in, 'inner', axis=0, tiled=True)]
    all_to_all x1 -> x0, blocking collectives: 247 us -> none  [on_device(): lax.all_to_all(outgoing, ('outer', 'inner'), split_axis=0, concat_axis=0,...]
    all_to_all x1 -> x0, waiting for transfers between devices: 229 us -> none  [on_device(): lax.all_to_all(jnp.einsum('sceh,ehj->scej', hidden, w_down, preferred_ele...]
    reshape x3 -> x1, local copies, waits for them, and re-layouts: 33.5 us -> 3.29 us  [on_device(): kv_rows = kv_all.reshape(-1, 4, HDIM)]
    gather x2 -> x0, local copies, waits for them, and re-layouts: 28.8 us -> none  [the longest x1 20.4 us: on_device(): returned.reshape(-1, D)[slot_index].reshape(row_count, MLP_TOP, D)]
    convert_element_type x1, local copies, waits for them, and re-layouts: 25.4 us -> 0.11 us  [on_device(): jnp.sum(att_weight[..., None] * value_all, axis=2).astype(BF)]
    dot_general x8 -> x6, matrix products: 28.3 us -> 6.74 us  [the longest x1 1.62 us: on_device(): jnp.einsum('tsk,snk->tn', normed.reshape(row_count, 4, 1024), router_all,...]
  transfers between devices with their start and end apart: 5 -> 0, of which waited for: 5 -> 0; matrix products, arithmetic and copies ran while one was open for 4% -> 0% of each run, Pallas kernels for 0% -> 0%
where the time goes in v1:
time: 622 us; the launch traced here: 616 us
  Pallas kernels  580 us (93%)
  local copies, waits for them, and re-layouts  22.6 us (4%)
  matrix products  6.74 us (1%)
  other arithmetic  6.43 us (1%)
    pallas_call x1, Pallas kernels, moe(): pl.pallas_call(moe_kernel, out_shape=(jax.ShapeDtypeStruct((ROWS, D), BF)...  508 us
    pallas_call x1, Pallas kernels, gather_att_in(): pl.pallas_call(att_in_kernel, out_shape=(jax.ShapeDtypeStruct((4, 1024, 7...  36.8 us
    pallas_call x1, Pallas kernels, gather_kv(): pl.pallas_call(kv_kernel, out_shape=(jax.ShapeDtypeStruct((8, 4, ROWS, 25...  35.8 us

profile of v1, /device:TPU:1, one launch (start us, length us, event | category | flops | bytes accessed | tf_op | source)
XLA Modules:
  0.0 616.5 jit_solution(6259453554846959429)
XLA Ops:
  0.0 1.7 fusion.3
  1.7 0.7 convert_reduce_fusion
  2.4 0.7 fusion.26
  3.3 1.2 iota_compare_fusion
  4.5 1.0 fusion.5
  5.5 36.8 %gather_att_in.1 = (bf16[4,1024,768]{2,1,0:T(8,128)(2,1)S(1)}, bf16[4,8,1024]{2,1,0:T(8,128)(2,1)S(1)}) custom-call(bf16[1024,768]{1,0:T(8,128)(2,1)S(1)} %copy-done.2, bf16[8,1024]{1,0:T(8,128)(2,1)S(1)} %bitcast.55), custom_call_target="tpu_custom_call" | custom-call | tf_op jit(solution)/shard_map/gather_att_in/pallas_call | solution.py:167
  42.3 1.1 fusion.29
  43.6 1.6 fusion.23
  45.5 1.2 copy-done.3
  46.8 35.8 %gather_kv.1 = (bf16[8,4,128,256]{3,2,1,0:T(8,128)(2,1)S(1)}, bf16[4,512,1024]{2,1,0:T(8,128)(2,1)S(1)}) custom-call(bf16[128,256]{1,0:T(8,128)(2,1)S(1)} %pad_maximum_fusion.kv, bf16[512,1024]{1,0:T(8,128)(2,1)S(1)} %copy-done.3), custom_call_target="tpu_custom_call" | custom-call | tf_op jit(solution)/shard_map/gather_kv/pallas_call | solution.py:224
  82.5 1.9 copy-done.1
  84.5 3.2 copy.36
  87.6 3.3 reshape.97
  91.0 6.3 %copy.38 = bf16[4,1024,512]{2,1,0:T(8,128)(2,1)} copy(bf16[4,1024,512]{1,2,0:T(8,128)(2,1)} %bitcast.53) | data formatting | bytes 8388608 | tf_op jit(solution)/shard_map/tk,skn->tsn/dot_general | solution.py:591
  97.2 1.1 fusion.30
  98.4 0.7 fusion.1
  99.1 0.9 multiply_reduce_fusion.2
  100.1 1.2 copy-done.6
  101.6 1.6 multiply_reduce_fusion
  103.5 0.4 fusion.27
  103.9 0.5 copy-done.5
  104.5 1.8 concatenate.7.ext
  106.3 507.9 %experts.1 = (bf16[128,4096]{1,0:T(8,128)(2,1)}, bf16[8,4096,256]{2,1,0:T(8,128)(2,1)}, bf16[8,256,4096]{2,1,0:T(8,128)(2,1)}) custom-call(bf16[128,4224]{1,0:T(8,128)(2,1)} %concatenate.7.ext, f32[128,4096]{1,0:T(8,128)} %copy-done.5, bf16[2,4096,256]{2,1,0:T(8,128)(2,1)} %up.1, bf16[2,256,4096]{2,1,0:T(8,128)(2,1)} %down.1), custom_call_target="tpu_custom_call" | custom-call | tf_op jit(solution)/shard_map/experts/pallas_call | solution.py:519
  614.2 2.3 copy.50
  (36 shorter events, 1.2 us)
Async XLA Ops:
  0.0 103.5 %copy-start = (bf16[4096,64]{0,1:T(8,128)(2,1)S(1)}, bf16[4096,64]{0,1:T(8,128)(2,1)}, u32[]{:S(2)}) copy-start(bf16[4096,64]{0,1:T(8,128)(2,1)} %param.19) | copy-start | bytes 1572868
  0.0 4.5 copy-start.7
  0.0 5.5 copy-start.4
  0.0 5.5 copy-start.2
  5.5 37.9 %copy-start.9 = (bf16[128,4096]{1,0:T(8,128)(2,1)}, bf16[128,4096]{1,0:T(8,128)(2,1)S(1)}, u32[]{:S(2)}) copy-start(bf16[128,4096]{1,0:T(8,128)(2,1)S(1)} %fusion.5) | copy-start | bytes 3145732
  45.5 1.2 copy-start.3
  82.5 1.9 copy-start.1
  90.9 6.3 %copy-start.10 = (pred[128,4096]{1,0:T(8,128)(4,1)S(1)}, pred[128,4096]{1,0:T(8,128)(4,1)}, u32[]{:S(2)}) copy-start(pred[128,4096]{1,0:T(8,128)(4,1)} %iota_compare_fusion) | copy-start | bytes 1572868
  99.1 2.2 copy-start.6
  99.1 2.5 copy-start.8
  101.6 1.6 copy-start.11
  103.1 1.3 copy-start.5

commit v2 on v1

--- a/solution.py
+++ b/solution.py
@@ -281,17 +281,33 @@
         for t in range(2):
             self.to_next(kind, m, t).start()
 
-    def turn(self, kind, m, after=None):
-        if after is not None:
-            self.begin(*after)
-        for t in range(3):
-            self.to_next(kind, m, t).wait_recv()
-            self.forward(kind, m, t).start()
-            self.sideways(kind, m, t, 0).start()
-            self.forward(kind, m, t).wait_recv()
-            self.sideways(kind, m, t, 1).start()
-            if t == 1:
-                self.to_next(kind, m, 2).start()
+    def take_far(self, kind, m, t):
+        self.to_next(kind, m, t).wait_recv()
+        self.forward(kind, m, t).start()
+        self.sideways(kind, m, t, 0).start()
+
+    def take_near(self, kind, m, t):
+        self.forward(kind, m, t).wait_recv()
+        self.sideways(kind, m, t, 1).start()
+
+    def turn(self, q, last, between=None):
+        kind, m = q // 4, q % 4
+        before = ((q - 1) // 4, (q - 1) % 4)
+        if q < last:
+            self.begin((q + 1) // 4, (q + 1) % 4)
+        if q <= last:
+            self.take_far(kind, m, 0)
+            self.take_far(kind, m, 1)
+        if q > 0:
+            self.take_far(*before, 2)
+        if between is not None:
+            between()
+        if q <= last:
+            self.take_near(kind, m, 0)
+            self.take_near(kind, m, 1)
+            self.to_next(kind, m, 2).start()
+        if q > 0:
+            self.take_near(*before, 2)
 
     def settle(self, kind, m):
         for t in range(3):
@@ -321,12 +337,6 @@
 ):
     p = Place()
     w = Weights(p, (up, down), (gup, gdn), (ns, fr, ps, sr, ys, yr))
-    own_copies = [
-        pltpu.make_async_copy(up, gup.at[pl.ds(2 * p.inner, 2)], local.at[0]),
-        pltpu.make_async_copy(down, gdn.at[pl.ds(2 * p.inner, 2)], local.at[1]),
-    ]
-    for copy in own_copies:
-        copy.start()
     meet(w.peers() + [p.along_x(1), p.along_x(2), p.along_x(3), p.sibling()])
     w.begin(0, 0)
 
@@ -357,33 +367,31 @@
     keep = pltpu.make_async_copy(ext, xall.at[p.outer], local.at[2])
     keep.start()
 
-    w.turn(0, 0, (0, 1))
-    mine(1, 0).wait_recv()
-    relay(1).start()
-    across(3, 0).start()
-    mine(3, 1).wait_recv()
-    relay(3).start()
-    across(1, 1).start()
-    mine(1, 1).wait_recv()
-    across(3, 1).start()
-    mine(3, 0).wait_recv()
-    across(1, 0).start()
-    w.turn(0, 1, (0, 2))
-    for d in (1, 3):
-        relay(d).wait_recv()
-        across(2, (d - 1) // 2).start()
-    for copy in own_copies:
-        copy.wait()
+    def loads(m, own, gathered, buffer, view):
+        for d in range(4):
+            two = pl.ds(2 * ((p.inner + d) % 4), 2)
+            src = view(own, slice(None)) if d == 0 else view(gathered, two)
+            yield pltpu.make_async_copy(src, buffer.at[m % 2, two], load.at[m % 2, d])
 
     def load_up(m):
-        return pltpu.make_async_copy(
-            gup.at[:, pl.ds(1024 * m, 1024), :], wbuf.at[m % 2], load.at[m % 2]
-        )
+        return loads(m, up, gup, wbuf, lambda ref, two: ref.at[two, pl.ds(1024 * m, 1024), :])
 
     def load_down(m):
-        return pltpu.make_async_copy(
-            gdn.at[:, :, pl.ds(1024 * m, 1024)], dbuf.at[m % 2], load.at[m % 2]
-        )
+        return loads(m, down, gdn, dbuf, lambda ref, two: ref.at[two, :, pl.ds(1024 * m, 1024)])
+
+    def fetch(q):
+        w.settle(q // 4, q % 4)
+        for copy in (load_up, load_down)[q // 4](q % 4):
+            copy.start()
+
+    def use(q):
+        for copy in (load_up, load_down)[q // 4](q % 4):
+            copy.wait()
+        if q < 4:
+            run_up(q)
+        else:
+            run_down(q - 4)
+            swap(q - 4).start()
 
     def run_up(m):
         xs = xall.at[:, :, pl.ds(1024 * m, 1024)]
@@ -445,60 +453,67 @@
             total += xbuf[m, d - 1].astype(F32)
         out[:, span] = total.astype(BF)
 
-    w.settle(0, 0)
-    load_up(0).start()
-    w.turn(0, 2, (0, 3))
-    keep.wait()
-    for d in range(4):
-        for h in range(2):
-            across(d, h).wait_recv()
-    w.settle(0, 1)
-    load_up(1).start()
-    load_up(0).wait()
-    run_up(0)
-    w.turn(0, 3, (1, 0))
-    w.settle(0, 2)
-    load_up(2).start()
-    load_up(1).wait()
-    run_up(1)
-    w.turn(1, 0, (1, 1))
-    w.settle(0, 3)
-    load_up(3).start()
-    load_up(2).wait()
-    run_up(2)
-    w.settle(1, 0)
-    load_down(0).start()
-    load_up(3).wait()
-    run_up(3)
-    gate()
-    w.turn(1, 1, (1, 2))
-    w.settle(1, 1)
-    load_down(1).start()
-    load_down(0).wait()
-    run_down(0)
-    swap(0).start()
-    w.turn(1, 2, (1, 3))
-    w.settle(1, 2)
-    load_down(2).start()
-    load_down(1).wait()
-    run_down(1)
-    swap(1).start()
-    add_pair(0)
-    w.turn(1, 3)
-    load_down(2).wait()
-    run_down(2)
-    swap(2).start()
+    def tokens_1():
+        mine(1, 0).wait_recv()
+        relay(1).start()
+        mine(3, 1).wait_recv()
+        relay(3).start()
+        across(3, 0).start()
+        across(1, 1).start()
+
+    def tokens_2():
+        mine(1, 1).wait_recv()
+        across(3, 1).start()
+        mine(3, 0).wait_recv()
+        across(1, 0).start()
+        for d in (1, 3):
+            relay(d).wait_recv()
+            across(2, (d - 1) // 2).start()
+        fetch(0)
+
+    def first_use():
+        keep.wait()
+        for d in range(4):
+            for h in range(2):
+                across(d, h).wait_recv()
+        use(0)
+        fetch(1)
+
+    def step_4():
+        use(1)
+        fetch(2)
+
+    def step_5():
+        use(2)
+        fetch(3)
+
+    def step_6():
+        use(3)
+        gate()
+        fetch(4)
+
+    def step_7():
+        use(4)
+        fetch(5)
+
+    def step_8():
+        add_pair(0)
+        use(5)
+        fetch(6)
+
+    steps = (None, tokens_1, tokens_2, first_use, step_4, step_5, step_6, step_7, step_8)
+    for q in range(9):
+        w.turn(q, 7, steps[q])
     add_pair(1)
+    use(6)
+    fetch(7)
     finish(0)
-    w.settle(1, 3)
-    load_down(3).start()
-    load_down(3).wait()
-    run_down(3)
-    swap(3).start()
     add_pair(2)
+    use(7)
+    finish(1)
     add_pair(3)
-    for m in (1, 2, 3):
-        finish(m)
+    finish(2)
+    finish(3)
     for kind in range(2):
         for m in range(4):
             w.drain(kind, m)
@@ -538,7 +553,7 @@
         + weight_sems()
         + [
             DMA((2, 2)), DMA((2, 2)), DMA((2,)), DMA((2,)), DMA((4, 2)), DMA((4, 2)),
-            DMA((4,)), DMA((4,)), DMA((4, 3)), DMA((4, 3)), DMA((3,)), DMA((2,)),
+            DMA((4,)), DMA((4,)), DMA((4, 3)), DMA((4, 3)), DMA((3,)), DMA((2, 4)),
         ],
         compiler_params=pltpu.CompilerParams(collective_id=3, has_side_effects=True, vmem_limit_bytes=60 * 2**20),
         name="experts",

time: 622 us -> 316 us (0.51)
  Pallas kernels: 580 us -> 279 us
    pallas_call x1, Pallas kernels: 508 us -> 207 us  [moe(): pl.pallas_call(moe_kernel, out_shape=(jax.ShapeDtypeStruct((ROWS, D), BF)...]
where the time goes in v2:
time: 316 us; the launch traced here: 315 us
  Pallas kernels  279 us (88%)
  local copies, waits for them, and re-layouts  22.6 us (7%)
  matrix products  6.75 us (2%)
  other arithmetic  6.43 us (2%)
    pallas_call x1, Pallas kernels, moe(): pl.pallas_call(moe_kernel, out_shape=(jax.ShapeDtypeStruct((ROWS, D), BF)...  207 us
    pallas_call x1, Pallas kernels, gather_att_in(): pl.pallas_call(att_in_kernel, out_shape=(jax.ShapeDtypeStruct((4, 1024, 7...  36.8 us
    pallas_call x1, Pallas kernels, gather_kv(): pl.pallas_call(kv_kernel, out_shape=(jax.ShapeDtypeStruct((8, 4, ROWS, 25...  35.8 us
    unnamed x25, local copies, waits for them, and re-layouts  7.48 us

profile of v2, /device:TPU:1, one launch (start us, length us, event | category | flops | bytes accessed | tf_op | source)
XLA Modules:
  0.0 315.1 jit_solution(10812746093750659813)
XLA Ops:
  0.0 1.7 fusion.3
  1.7 0.7 convert_reduce_fusion
  2.4 0.7 fusion.26
  3.3 1.2 iota_compare_fusion
  4.5 1.0 fusion.5
  5.5 36.8 %gather_att_in.1 = (bf16[4,1024,768]{2,1,0:T(8,128)(2,1)S(1)}, bf16[4,8,1024]{2,1,0:T(8,128)(2,1)S(1)}) custom-call(bf16[1024,768]{1,0:T(8,128)(2,1)S(1)} %copy-done.2, bf16[8,1024]{1,0:T(8,128)(2,1)S(1)} %bitcast.55), custom_call_target="tpu_custom_call" | custom-call | tf_op jit(solution)/shard_map/gather_att_in/pallas_call | solution.py:167
  42.3 1.1 fusion.29
  43.6 1.6 fusion.23
  45.5 1.2 copy-done.3
  46.8 35.8 %gather_kv.1 = (bf16[8,4,128,256]{3,2,1,0:T(8,128)(2,1)S(1)}, bf16[4,512,1024]{2,1,0:T(8,128)(2,1)S(1)}) custom-call(bf16[128,256]{1,0:T(8,128)(2,1)S(1)} %pad_maximum_fusion.kv, bf16[512,1024]{1,0:T(8,128)(2,1)S(1)} %copy-done.3), custom_call_target="tpu_custom_call" | custom-call | tf_op jit(solution)/shard_map/gather_kv/pallas_call | solution.py:224
  82.5 1.9 copy-done.1
  84.5 3.2 %copy.36 = bf16[8,4,128,256]{2,1,0,3:T(4,128)(2,1)} copy(bf16[8,4,128,256]{3,2,1,0:T(8,128)(2,1)S(1)} %get-tuple-element.12) | data formatting | bytes 4194304 | tf_op jit(solution)/shard_map/gather_kv/pallas_call | solution.py:224
  87.6 3.3 %reshape.97 = bf16[4096,4,64]{0,2,1:T(8,128)(2,1)S(1)} reshape(bf16[8,4,128,256]{2,1,0,3:T(4,128)(2,1)} %copy.36) | data formatting | bytes 4194304 | tf_op jit(solution)/shard_map/reshape | solution.py:593
  91.0 6.3 %copy.38 = bf16[4,1024,512]{2,1,0:T(8,128)(2,1)} copy(bf16[4,1024,512]{1,2,0:T(8,128)(2,1)} %bitcast.53) | data formatting | bytes 8388608 | tf_op jit(solution)/shard_map/tk,skn->tsn/dot_general | solution.py:606
  97.2 1.1 fusion.30
  98.4 0.7 fusion.1
  99.1 0.9 multiply_reduce_fusion.2
  100.1 1.2 copy-done.6
  101.6 1.6 multiply_reduce_fusion
  103.5 0.4 fusion.27
  103.9 0.5 copy-done.5
  104.5 1.8 concatenate.7.ext
  106.3 206.5 %experts.1 = (bf16[128,4096]{1,0:T(8,128)(2,1)}, bf16[8,4096,256]{2,1,0:T(8,128)(2,1)}, bf16[8,256,4096]{2,1,0:T(8,128)(2,1)}) custom-call(bf16[128,4224]{1,0:T(8,128)(2,1)} %concatenate.7.ext, f32[128,4096]{1,0:T(8,128)} %copy-done.5, bf16[2,4096,256]{2,1,0:T(8,128)(2,1)} %up.1, bf16[2,256,4096]{2,1,0:T(8,128)(2,1)} %down.1), custom_call_target="tpu_custom_call" | custom-call | tf_op jit(solution)/shard_map/experts/pallas_call | solution.py:534
  312.8 2.3 copy.50
  (36 shorter events, 1.2 us)
Async XLA Ops:
  0.0 103.5 %copy-start = (bf16[4096,64]{0,1:T(8,128)(2,1)S(1)}, bf16[4096,64]{0,1:T(8,128)(2,1)}, u32[]{:S(2)}) copy-start(bf16[4096,64]{0,1:T(8,128)(2,1)} %param.19) | copy-start | bytes 1572868
  0.0 4.5 %copy-start.7 = (bf16[128,4096]{1,0:T(8,128)(2,1)S(1)}, bf16[128,4096]{1,0:T(8,128)(2,1)}, u32[]{:S(2)}) copy-start(bf16[128,4096]{1,0:T(8,128)(2,1)} %param.11) | copy-start | bytes 3145732
  0.0 5.5 %copy-start.4 = (bf16[1024,8]{0,1:T(8,128)(2,1)S(1)}, bf16[1024,8]{0,1:T(8,128)(2,1)}, u32[]{:S(2)}) copy-start(bf16[1024,8]{0,1:T(8,128)(2,1)} %param.16) | copy-start | bytes 49156
  0.0 5.5 %copy-start.2 = (bf16[1024,768]{1,0:T(8,128)(2,1)S(1)}, bf16[1024,768]{1,0:T(8,128)(2,1)}, u32[]{:S(2)}) copy-start(bf16[1024,768]{1,0:T(8,128)(2,1)} %w.2) | copy-start | bytes 4718596
  5.5 37.9 %copy-start.9 = (bf16[128,4096]{1,0:T(8,128)(2,1)}, bf16[128,4096]{1,0:T(8,128)(2,1)S(1)}, u32[]{:S(2)}) copy-start(bf16[128,4096]{1,0:T(8,128)(2,1)S(1)} %fusion.5) | copy-start | bytes 3145732
  45.5 1.2 copy-start.3
  82.5 1.9 copy-start.1
  90.9 6.3 %copy-start.10 = (pred[128,4096]{1,0:T(8,128)(4,1)S(1)}, pred[128,4096]{1,0:T(8,128)(4,1)}, u32[]{:S(2)}) copy-start(pred[128,4096]{1,0:T(8,128)(4,1)} %iota_compare_fusion) | copy-start | bytes 1572868
  99.1 2.2 copy-start.6
  99.1 2.5 copy-start.8
  101.6 1.6 copy-start.11
  103.1 1.3 copy-start.5

commit v3 on v2

v3 whole, which is shorter than its diff:
```python
import functools

import jax
import jax.numpy as jnp
from jax import lax
from jax.experimental import pallas as pl
from jax.experimental.pallas import tpu as pltpu
from jax.sharding import PartitionSpec as P

D = 4096
HEADS = 2
HDIM = 64
ATT_EXP = 4
EXT = D + 128
ROWS = 128
EARLY = 4
epsilon = 1e-05
MESH = pl.DeviceIdType.MESH
ANY = pl.BlockSpec(memory_space=pl.ANY)
VM = pl.BlockSpec(memory_space=pltpu.VMEM)
DMA = pltpu.SemaphoreType.DMA
BF = jnp.bfloat16
F32 = jnp.float32


class Place:
    def __init__(self):
        self.seq, self.outer, self.inner = (lax.axis_index(a) for a in ("seq", "outer", "inner"))
        self.zl, self.y = self.seq // 4, self.seq % 4
        self.x, self.c = self.outer // 2, self.outer % 2

    def along_z(self, d):
        return (self.seq, self.outer, (self.inner + d) % 4)

    def along_y(self, d):
        return (self.zl * 4 + (self.y + d) % 4, self.outer, self.inner)

    def along_x(self, d):
        return (self.seq, ((self.x + d) % 4) * 2 + self.c, self.inner)

    def sibling(self):
        return (self.seq, self.x * 2 + 1 - self.c, self.inner)

    def pair(self):
        return ((1 - self.zl) * 4 + self.y, self.outer, self.inner)

    def beyond(self):
        return ((1 - self.zl) * 4 + self.y, self.outer, (self.inner + 2 * self.zl - 1) % 4)


def meet(peers):
    barrier = pltpu.get_barrier_semaphore()
    for peer in peers:
        pl.semaphore_signal(barrier, inc=1, device_id=peer, device_id_type=MESH)
    pl.semaphore_wait(barrier, len(peers))


def remote(src, dst, send, recv, peer):
    return pltpu.make_async_remote_copy(
        src_ref=src, dst_ref=dst, send_sem=send, recv_sem=recv, device_id=peer, device_id_type=MESH
    )


def spread_over_z(at, own, gathered, full, p, sems):
    s1, r1, s2, r2, s3, r3 = sems
    n = full // 16
    spans = (
        pl.ds(pl.multiple_of(p.c * (4 * n) + p.y * n, n), n),
        pl.ds(pl.multiple_of(8 * n + p.c * (4 * n) + p.x * n, n), n),
    )
    halves = tuple(pl.ds(pl.multiple_of(8 * n * h + p.c * (4 * n), 4 * n), 4 * n) for h in range(2))

    def first(d, h):
        return remote(
            own.at[spans[h]], gathered.at[p.inner, spans[h]], s1.at[at, d - 1, h], r1.at[at, d - 1, h], p.along_z(d)
        )

    def second(d, h, e):
        j = (p.inner - d + 4) % 4
        peer = p.along_y(e) if h == 0 else p.along_x(e)
        block = gathered.at[j, spans[h]]
        return remote(block, block, s2.at[at, d - 1, h, e - 1], r2.at[at, d - 1, h, e - 1], peer)

    def third(d, h):
        j = (p.inner - d + 4) % 4
        block = gathered.at[j, halves[h]]
        return remote(block, block, s3.at[at, d - 1, h], r3.at[at, d - 1, h], p.sibling())

    order = (1, 3, 2)
    every = [(d, h) for d in order for h in range(2)]

    def go1():
        for d, h in every:
            first(d, h).start()

    def go2(d):
        for h in range(2):
            first(d, h).wait_recv()
            for e in (1, 3, 2):
                second(d, h, e).start()

    def go3(d):
        for h in range(2):
            for e in (1, 3, 2):
                second(d, h, e).wait_recv()
            third(d, h).start()

    def arrived():
        for d, h in every:
            third(d, h).wait_recv()

    def sent():
        for d, h in every:
            first(d, h).wait_send()
            third(d, h).wait_send()
            for e in (1, 3, 2):
                second(d, h, e).wait_send()

    return order, go1, go2, go3, arrived, sent


def spread_sems(n):
    return [DMA((n, 3, 2)), DMA((n, 3, 2)), DMA((n, 3, 2, 3)), DMA((n, 3, 2, 3)), DMA((n, 3, 2)), DMA((n, 3, 2))]


def square_peers(p):
    return (
        [p.along_z(d) for d in (1, 2, 3)]
        + [p.along_y(d) for d in (1, 2, 3)]
        + [p.along_x(d) for d in (1, 2, 3)]
        + [p.sibling()]
    )


class Weights:
    def __init__(self, p, steps, sems):
        self.p, self.steps = p, steps
        self.ns, self.fr, self.ps, self.sr, self.ys, self.yr = sems
        self.k = p.y % 2
        self.way = 2 * p.zl - 1
        self.done = 0

    def part(self, ref, up, e, c):
        span = pl.ds(pl.multiple_of(c * 256, 256), 256)
        return ref.at[e, span, :] if up else ref.at[e, :, span]

    def chunk(self, i, shard, c):
        _, gathered, up, _, base = self.steps[i]
        return self.part(gathered, up, ((shard + 8) % 4) * 2 + self.k, base + c)

    def to_next(self, i, t):
        p = self.p
        own, _, up, base, _ = self.steps[i]
        if t < 2:
            src = self.part(own, up, self.k, base + t)
            dst = self.chunk(i, p.inner, t)
        else:
            src = dst = self.chunk(i, p.inner - self.way, 1 - p.zl)
        return remote(src, dst, self.ns.at[i, t], self.fr.at[i, t], p.beyond())

    def far(self, t):
        p = self.p
        return (p.inner + self.way, t) if t < 2 else (p.inner + 2, p.zl)

    def near(self, t):
        p = self.p
        return (p.inner - self.way, t) if t < 2 else (p.inner + 2, 1 - p.zl)

    def forward(self, i, t):
        block = self.chunk(i, *self.far(t))
        return remote(block, block, self.ps.at[i, t], self.sr.at[i, t], self.p.pair())

    def sideways(self, i, t, which):
        shard, c = (self.far, self.near)[which](t)
        block = self.chunk(i, shard, c)
        peer = self.p.along_y(5 - 2 * (c % 2))
        return remote(block, block, self.ys.at[i, t, which], self.yr.at[i, t, which], peer)

    def begin(self, i):
        for t in range(2):
            self.to_next(i, t).start()

    def take_far(self, i, t):
        self.to_next(i, t).wait_recv()
        self.forward(i, t).start()
        self.sideways(i, t, 0).start()

    def take_near(self, i, t):
        self.forward(i, t).wait_recv()
        self.sideways(i, t, 1).start()

    def turn(self, i):
        n = len(self.steps)
        if i < n - 1:
            self.begin(i + 1)
        if i < n:
            self.take_far(i, 0)
            self.take_far(i, 1)
        if 0 <= i - 2 < n:
            self.take_far(i - 2, 2)
        if 0 <= i - 1 < n:
            self.take_near(i - 1, 0)
            self.take_near(i - 1, 1)
            self.to_next(i - 1, 2).start()
        if 0 <= i - 3 < n:
            self.take_near(i - 3, 2)

    def advance(self, to):
        for i in range(self.done, min(max(to, self.done) + 1, len(self.steps) + 3)):
            self.turn(i)
            self.done = i + 1

    def settle(self, i):
        for t in range(3):
            for which in range(2):
                self.sideways(i, t, which).wait_recv()

    def drain(self):
        for i in range(len(self.steps)):
            for t in range(3):
                self.to_next(i, t).wait_send()
                self.forward(i, t).wait_send()
                for which in range(2):
                    self.sideways(i, t, which).wait_send()

    def peers(self):
        p = self.p
        return [p.beyond(), p.pair(), p.along_y(1), p.along_y(3)]


def weight_sems(n):
    return [DMA((n, 3))] * 4 + [DMA((n, 3, 2))] * 2


def across_rows(a, b):
    return lax.dot_general(a, b, (((1,), (1,)), ((), ())), preferred_element_type=F32)


def norm_rows(src, gain, dst):
    def one(r, carry):
        rows = pl.ds(pl.multiple_of(16 * r, 16), 16)
        floats = src[rows, :].astype(F32)
        scale = lax.rsqrt(jnp.mean(floats * floats, axis=-1, keepdims=True) + epsilon)
        dst[rows, 0:D] = (floats * scale * gain[...]).astype(BF)
        return carry

    lax.fori_loop(0, 8, one, 0)


def attention_kernel(
    tok, gain, mlp_gain, chosen, picked, mlp_router, w_in, router, w_out, up, ext, hs, gup,
    normed, gw, gr, kv, gk, ao,
    s1, r1, s2, r2, s3, r3, ro_s, ro_r, sz, rz, sx, rx, sc, rc, local, ns, fr, ps, sr, ys, yr,
):
    p = Place()
    steps = [(up, gup, True, 2 * m, 2 * m) for m in range(2 * EARLY)]
    w = Weights(p, steps, (ns, fr, ps, sr, ys, yr))
    own = [
        pltpu.make_async_copy(w_in, gw.at[p.inner], local.at[0]),
        pltpu.make_async_copy(router, gr.at[p.inner], local.at[1]),
        pltpu.make_async_copy(w_out, ao.at[p.inner], local.at[2]),
    ]
    for copy in own:
        copy.start()
    meet(square_peers(p) + [p.beyond(), p.pair()])
    sems = (s1, r1, s2, r2, s3, r3)
    order, in1, in2, in3, in_arrived, in_sent = spread_over_z(0, w_in, gw, 1024, p, sems)
    _, out1, out2, out3, out_arrived, out_sent = spread_over_z(1, w_out, ao, 512, p, sems)
    routers = [remote(router, gr.at[p.inner], ro_s.at[d - 1], ro_r.at[d - 1], p.along_z(d)) for d in (1, 2, 3)]
    zs = [remote(kv, gk.at[p.outer, p.inner], sz.at[d - 1], rz.at[d - 1], p.along_z(d)) for d in (1, 2, 3)]
    xs = [remote(gk.at[p.outer], gk.at[p.outer], sx.at[d - 1], rx.at[d - 1], p.along_x(d)) for d in (1, 2, 3)]
    cs = []
    for d in range(4):
        o = ((p.x - d + 4) % 4) * 2 + p.c
        cs.append(remote(gk.at[o], gk.at[o], sc.at[d], rc.at[d], p.sibling()))

    in1()
    for copy in routers:
        copy.start()
    norm_rows(tok, gain, normed)
    for d in order:
        in2(d)
    w.begin(0)
    for d in order:
        in3(d)
    w.advance(0)
    in_arrived()
    w.advance(1)
    for copy in routers:
        copy.wait_recv()
    own[0].wait()
    own[1].wait()

    proj = jnp.zeros((ROWS, 768), F32)
    logit = jnp.zeros((ROWS, 8), F32)
    for j in range(4):
        piece = normed[:, 1024 * j : 1024 * (j + 1)]
        proj += jnp.dot(piece, gw[j], preferred_element_type=F32)
        logit += across_rows(piece, gr[j])
    weight = jax.nn.sigmoid(logit) * chosen[...]
    mixes = []
    for h in range(HEADS):
        mix = jnp.zeros((ROWS, HDIM), F32)
        for e in range(4 * h, 4 * h + 4):
            mix += weight[:, e : e + 1] * proj[:, 256 + HDIM * e : 256 + HDIM * (e + 1)]
        mixes.append(mix)
    kv[:, 0:128] = proj[:, 128:256].astype(BF)
    kv[:, 128:256] = jnp.concatenate(mixes, axis=1).astype(BF)
    query = proj[:, 0:128].astype(BF)
    for copy in zs:
        copy.start()
    keep = pltpu.make_async_copy(kv, gk.at[p.outer, p.inner], local.at[3])
    keep.start()
    out1()
    w.advance(2)
    keep.wait()
    for copy in zs:
        copy.wait_recv()
    for copy in (xs[0], xs[2], xs[1]):
        copy.start()
    cs[0].start()
    for d in order:
        out2(d)
    w.advance(3)
    for d in (1, 3, 2):
        xs[d - 1].wait_recv()
        cs[d].start()
    for d in order:
        out3(d)
    w.advance(4)
    for copy in cs:
        copy.wait_recv()

    place = (p.outer * 4 + p.inner) * ROWS + lax.broadcasted_iota(jnp.int32, (ROWS, 512), 0)
    spot = lax.broadcasted_iota(jnp.int32, (ROWS, 512), 1)
    heads = []
    for h in range(HEADS):
        mine = query[:, HDIM * h : HDIM * (h + 1)]

        def one(o, carry):
            top, total, out = carry
            held = gk[o].reshape(512, 256)
            scores = across_rows(mine, held[:, HDIM * h : HDIM * (h + 1)]) * HDIM ** (-0.5)
            scores = jnp.where(spot + 512 * o <= place, scores, -1e30)
            high = jnp.maximum(top, jnp.max(scores, axis=-1, keepdims=True))
            shares = jnp.exp(scores - high)
            fade = jnp.exp(top - high)
            values = held[:, 128 + HDIM * h : 128 + HDIM * (h + 1)]
            return (
                high,
                total * fade + jnp.sum(shares, axis=-1, keepdims=True),
                out * fade + jnp.dot(shares.astype(BF), values, preferred_element_type=F32),
            )

        start = (
            jnp.full((ROWS, 1), -1e30, F32),
            jnp.zeros((ROWS, 1), F32),
            jnp.zeros((ROWS, HDIM), F32),
        )
        _, total, out = lax.fori_loop(0, p.outer + 1, one, start)
        out = out / total
        heads.append(out * lax.rsqrt(jnp.mean(out * out, axis=-1, keepdims=True) + epsilon))
        w.advance(0)
    mixed = jnp.concatenate([weight[:, e : e + 1] * heads[e // 4] for e in range(8)], axis=1).astype(BF)
    out_arrived()
    own[2].wait()
    for j in range(4):
        span = slice(1024 * j, 1024 * (j + 1))
        hs[:, span] = tok[:, span].astype(F32) + jnp.dot(mixed, ao[j], preferred_element_type=F32)
    w.advance(0)
    norm_rows(hs, mlp_gain, ext)
    gates = jax.nn.sigmoid(across_rows(ext[:, 0:D], mlp_router[...])) * picked[...]
    high = gates.astype(BF)
    ext[:, D:] = jnp.concatenate([high, (gates - high.astype(F32)).astype(BF)], axis=1)
    w.advance(99)
    for i in range(2 * EARLY):
        w.settle(i)
    w.drain()
    in_sent()
    out_sent()
    for copy in routers + zs + xs + cs:
        copy.wait_send()


def attention(*arrays):
    return pl.pallas_call(
        attention_kernel,
        out_shape=(
            jax.ShapeDtypeStruct((ROWS, EXT), BF),
            jax.ShapeDtypeStruct((ROWS, D), F32),
            jax.ShapeDtypeStruct((8, EARLY * 1024, 256), BF),
        ),
        in_specs=[VM] * 6 + [ANY] * 4,
        out_specs=(VM, VM, ANY),
        scratch_shapes=[
            pltpu.VMEM((ROWS, D), BF),
            pltpu.VMEM((4, 1024, 768), BF),
            pltpu.VMEM((4, 8, 1024), BF),
            pltpu.VMEM((ROWS, 256), BF),
            pltpu.VMEM((8, 4, ROWS, 256), BF),
            pltpu.VMEM((4, 512, 1024), BF),
        ]
        + spread_sems(2)
        + [DMA((3,))] * 6
        + [DMA((4,))] * 3
        + weight_sems(2 * EARLY),
        compiler_params=pltpu.CompilerParams(collective_id=1, has_side_effects=True, vmem_limit_bytes=60 * 2**20),
        name="attention",
    )(*arrays)


def moe_kernel(
    ext, hs, up, early, down, out, late, gdn,
    xall, acc, hid, wbuf, dbuf, part, pairbuf, xbuf,
    ns, fr, ps, sr, ys, yr, ts, tr, us, ur, vs, vr, es, er, qs, qr, local, load,
):
    p = Place()
    steps = [(up, late, True, 2 * m, 2 * m - 4 * EARLY) for m in range(2 * EARLY, 8)]
    steps += [(down, gdn, False, 2 * m, 2 * m) for m in range(8)]
    w = Weights(p, steps, (ns, fr, ps, sr, ys, yr))
    meet(w.peers() + [p.along_x(1), p.along_x(2), p.along_x(3), p.sibling()])
    def rows(o, h):
        return xall.at[o, pl.ds(64 * h, 64), :]

    def block(d):
        return ((p.x + d) % 4) * 2 + p.c

    def mine(d, h):
        src = ext.at[pl.ds(64 * h, 64), :]
        return remote(src, rows(p.outer, h), ts.at[(d - 1) // 2, h], tr.at[(d - 1) // 2, h], p.along_x(d))

    def relay(d):
        h = (d - 1) // 2
        src = rows(block(4 - d), h)
        return remote(src, src, us.at[h], ur.at[h], p.along_x(d))

    def across(d, h):
        src = ext.at[pl.ds(64 * h, 64), :] if d == 0 else rows(block(d), h)
        return remote(src, rows(block(d), h), vs.at[d, h], vr.at[d, h], p.sibling())

    for h in range(2):
        for d in (1, 3):
            mine(d, h if d == 1 else 1 - h).start()
    for h in range(2):
        across(0, h).start()
    keep = pltpu.make_async_copy(ext, xall.at[p.outer], local.at[2])
    keep.start()
    w.begin(0)

    def loads(own, gathered, buffer, at):
        for d in range(4):
            two = pl.ds(2 * ((p.inner + d) % 4), 2)
            src = own if d == 0 else gathered.at[two]
            yield pltpu.make_async_copy(src, buffer.at[two], load.at[at, d])

    def load_up(m):
        held, base = (early, 0) if m < EARLY else (late, EARLY)
        mine_up = up.at[:, pl.ds(1024 * m, 1024), :]
        return loads(mine_up, held.at[:, pl.ds(1024 * (m - base), 1024), :], wbuf.at[m % 3], m % 3)

    def load_down(m):
        span = pl.ds(1024 * m, 1024)
        return loads(down.at[:, :, span], gdn.at[:, :, span], dbuf.at[m % 2], 3 + m % 2)

    def fetch(copies):
        for copy in copies:
            copy.start()

    def land(copies):
        for copy in copies:
            copy.wait()

    def run_up(m, groups):
        for d in groups:
            there = (p.x + d) % 4

            def one(e, carry):
                tokens = xall[pl.ds(2 * there, 2), :, pl.ds(1024 * m, 1024)].reshape(256, 1024)
                rows = pl.ds(pl.multiple_of(256 * there, 256), 256)
                got = jnp.dot(tokens, wbuf[m % 3, e], preferred_element_type=F32)
                if m == 0:
                    acc[e, rows, :] = got
                else:
                    acc[e, rows, :] += got
                return carry

            lax.fori_loop(0, 8, one, 0)

    def run_up_all(m):
        def one(e, carry):
            tokens = xall[:, :, pl.ds(1024 * m, 1024)].reshape(1024, 1024)
            acc[e] += jnp.dot(tokens, wbuf[m % 3, e], preferred_element_type=F32)
            return carry

        lax.fori_loop(0, 8, one, 0)

    def gate():
        names = lax.broadcasted_iota(jnp.int32, (128, 256), 0) % 64
        shares = xall[:, :, D:].reshape(1024, 128)

        def one(e, carry):
            pick = jnp.where(names == p.outer * 8 + e, 1.0, 0.0).astype(BF)
            scale = jnp.dot(shares, pick, preferred_element_type=F32)
            hid[:, pl.ds(pl.multiple_of(256 * e, 256), 256)] = (jnp.maximum(acc[e], 0.0) * scale).astype(BF)
            return carry

        lax.fori_loop(0, 8, one, 0)

    def run_down(m):
        def one(n, carry):
            span = pl.ds(pl.multiple_of(256 * n, 256), 256)
            weights = dbuf[m % 2, :, :, span].reshape(2048, 256)
            got = jnp.dot(hid[...], weights, preferred_element_type=F32)
            part[m, :, :, :, span] = got.astype(BF).reshape(4, 2, 128, 256)
            return carry

        lax.fori_loop(0, 4, one, 0)

    def swap(m):
        return remote(part.at[m, :, 1 - p.c], pairbuf.at[m], es.at[m], er.at[m], p.sibling())

    def give(m, d):
        there = (p.x + d) % 4
        return remote(part.at[m, there, p.c], xbuf.at[m, d - 1], qs.at[m, d - 1], qr.at[m, d - 1], p.along_x(d))

    def add_pair(m):
        swap(m).wait_recv()
        for d in (1, 3, 2):
            there = (p.x + d) % 4
            total = part[m, there, p.c].astype(F32) + pairbuf[m, there].astype(F32)
            part[m, there, p.c] = total.astype(BF)
            give(m, d).start()

    def finish(m):
        span = pl.ds(1024 * m, 1024)
        total = hs[:, span] + part[m, p.x, p.c].astype(F32) + pairbuf[m, p.x].astype(F32)
        for d in (1, 3, 2):
            give(m, d).wait_recv()
            total += xbuf[m, d - 1].astype(F32)
        out[:, span] = total.astype(BF)

    def from_sibling(d):
        for h in range(2):
            across(d, h).wait_recv()

    def part_0():
        mine(1, 0).wait_recv()
        relay(1).start()
        mine(3, 1).wait_recv()
        relay(3).start()
        across(3, 0).start()
        across(1, 1).start()
        keep.wait()
        from_sibling(0)
        for m in range(2):
            land(load_up(m))
            run_up(m, (0,))

    def part_1():
        mine(1, 1).wait_recv()
        across(3, 1).start()
        mine(3, 0).wait_recv()
        across(1, 0).start()
        from_sibling(1)
        from_sibling(3)
        for m in range(2):
            run_up(m, (1, 3))

    def part_2():
        for d in (1, 3):
            relay(d).wait_recv()
            across(2, (d - 1) // 2).start()
        if EARLY > 2:
            fetch(load_up(2))
        from_sibling(2)
        for m in range(2):
            run_up(m, (2,))
        if EARLY > 3:
            fetch(load_up(3))

    def rest_up(m):
        if m >= EARLY:
            w.settle(2 * (m - EARLY))
            w.settle(2 * (m - EARLY) + 1)
            fetch(load_up(m))
        land(load_up(m))
        run_up_all(m)
        if m == 3:
            gate()

    def produce(m):
        w.settle(2 * (4 - EARLY + m))
        w.settle(2 * (4 - EARLY + m) + 1)
        fetch(load_down(m))
        if m > 0:
            add_pair(m - 1)
        if m > 1:
            finish(m - 2)
        land(load_down(m))
        run_down(m)
        swap(m).start()

    fetch(load_up(0))
    fetch(load_up(1))
    w.advance(0)
    part_0()
    w.advance(2)
    part_1()
    w.advance(3)
    part_2()
    for m in (2, 3):
        w.advance(2 * (m - EARLY) + 4 if m >= EARLY else 0)
        rest_up(m)
    for m in range(4):
        w.advance(2 * (4 - EARLY + m) + 4)
        produce(m)
    add_pair(3)
    finish(2)
    finish(3)
    w.drain()
    for h in range(2):
        for d in (1, 3):
            mine(d, h).wait_send()
        for d in range(4):
            across(d, h).wait_send()
    for d in (1, 3):
        relay(d).wait_send()
    for m in range(4):
        swap(m).wait_send()
        for d in (1, 2, 3):
            give(m, d).wait_send()


def moe(ext, hidden_state, w_up, gathered_up, w_down):
    return pl.pallas_call(
        moe_kernel,
        out_shape=(
            jax.ShapeDtypeStruct((ROWS, D), BF),
            jax.ShapeDtypeStruct((8, max(1, 4 - EARLY) * 1024, 256), BF),
            jax.ShapeDtypeStruct((8, 256, D), BF),
        ),
        in_specs=[ANY, VM, ANY, ANY, ANY],
        out_specs=(VM, ANY, ANY),
        scratch_shapes=[
            pltpu.VMEM((8, ROWS, EXT), BF),
            pltpu.VMEM((8, 1024, 256), F32),
            pltpu.VMEM((1024, 2048), BF),
            pltpu.VMEM((3, 8, 1024, 256), BF),
            pltpu.VMEM((2, 8, 256, 1024), BF),
            pltpu.VMEM((4, 4, 2, ROWS, 1024), BF),
            pltpu.VMEM((4, 4, ROWS, 1024), BF),
            pltpu.VMEM((4, 3, ROWS, 1024), BF),
        ]
        + weight_sems(16 - 2 * EARLY)
        + [
            DMA((2, 2)), DMA((2, 2)), DMA((2,)), DMA((2,)), DMA((4, 2)), DMA((4, 2)),
            DMA((4,)), DMA((4,)), DMA((4, 3)), DMA((4, 3)), DMA((3,)), DMA((5, 4)),
        ],
        compiler_params=pltpu.CompilerParams(collective_id=3, has_side_effects=True, vmem_limit_bytes=60 * 2**20),
        name="experts",
    )(ext, hidden_state, w_up, gathered_up, w_down)[0]


def on_device(
    tokens,
    att_ids,
    mlp_ids,
    att_gain,
    att_in,
    att_router,
    att_out,
    mlp_gain,
    mlp_router,
    w_up,
    w_down,
):
    row_count = tokens.shape[0]
    chosen = jnp.any(att_ids[..., None] == jnp.arange(ATT_EXP)[None, None, None, :], axis=2)
    picked = jnp.any(mlp_ids[..., None] == jnp.arange(mlp_router.shape[1])[None, None, :], axis=1)
    ext, hidden_state, gathered_up = attention(
        tokens,
        att_gain[None, :],
        mlp_gain[None, :],
        chosen.reshape(row_count, HEADS * ATT_EXP).astype(F32),
        picked.astype(F32),
        mlp_router.T,
        att_in,
        att_router.T,
        att_out,
        w_up,
    )
    return moe(ext, hidden_state, w_up, gathered_up, w_down)


def solution(mesh):
    in_specs = (
        P(("seq", "outer", "inner"), None),
        P(("seq", "outer", "inner"), None, None),
        P(("seq", "outer", "inner"), None),
        P(),
        P("inner", None),
        P("inner", None),
        P(None, "inner"),
        P(),
        P(),
        P(("outer", "inner"), None, None),
        P(("outer", "inner"), None, None),
    )
    out_specs = P(("seq", "outer", "inner"), None)
    return jax.shard_map(
        on_device, mesh=mesh, in_specs=in_specs, out_specs=out_specs, check_vma=False
    )
```

time: 316 us -> 287 us (0.908)
  local copies, waits for them, and re-layouts: 22.6 us -> 3.73 us
  matrix products: 6.75 us -> 0 us
  other arithmetic: 6.43 us -> 1.44 us
    pallas_call x2 -> x1, Pallas kernels: 72.5 us -> 135 us  [attention(): pl.pallas_call(attention_kernel, out_shape=(jax.ShapeDtypeStruct((ROWS, E...]
    pallas_call x1, Pallas kernels: 207 us -> 147 us  [moe(): pl.pallas_call(moe_kernel, out_shape=(jax.ShapeDtypeStruct((ROWS, D), BF)...]
    dot_general x6 -> x0, matrix products: 6.75 us -> none  [the longest x1 1.62 us: on_device(): jnp.einsum('tsk,snk->tn', normed.reshape(row_count, 4, 1024), router_all,...]
    dot_general x2 -> x0, local copies, waits for them, and re-layouts: 6.3 us -> none  [the longest x1 6.27 us: on_device(): jnp.einsum('tk,skn->tsn', mixed, out_all, preferred_element_type=F32)]
    unnamed x25 -> x1, local copies, waits for them, and re-layouts: 7.48 us -> 2.29 us
    reshape x1 -> x0, local copies, waits for them, and re-layouts: 3.29 us -> none  [on_device(): kv_rows = kv_all.reshape(-1, 4, HDIM)]
    pallas_call x1 -> x0, local copies, waits for them, and re-layouts: 3.19 us -> none  [gather_kv(): pl.pallas_call(kv_kernel, out_shape=(jax.ShapeDtypeStruct((8, 4, ROWS, 25...]
where the time goes in v3:
time: 287 us
  Pallas kernels  282 us (98%)
  local copies, waits for them, and re-layouts  3.73 us (1%)
    pallas_call x1, Pallas kernels, moe(): pl.pallas_call(moe_kernel, out_shape=(jax.ShapeDtypeStruct((ROWS, D), BF)...  147 us
    pallas_call x1, Pallas kernels, attention(): pl.pallas_call(attention_kernel, out_shape=(jax.ShapeDtypeStruct((ROWS, E...  135 us

profile of v3, /device:TPU:1, one launch (start us, length us, event | category | flops | bytes accessed | tf_op | source)
XLA Modules:
  0.0 286.7 jit_solution(10759976567386978187)
XLA Ops:
  0.0 0.7 fusion.1
  0.7 0.7 fusion
  1.5 0.7 copy.20.picked
  2.2 0.7 copy.19.chosen
  2.9 134.8 %attention.1 = (bf16[128,4224]{1,0:T(8,128)(2,1)}, f32[128,4096]{1,0:T(8,128)}, bf16[8,4096,256]{2,1,0:T(8,128)(2,1)}) custom-call(bf16[128,4096]{1,0:T(8,128)(2,1)} %tok.1, f32[1,4096]{1,0:T(1,128)} %bitcast.6, f32[1,4096]{1,0:T(1,128)} %bitcast.7, f32[128,8]{1,0:T(8,128)} %copy.19.chosen, f32[128,64]{1,0:T(8,128)} %copy.20.picked, ...), custom_call_target="tpu_custom_call" | custom-call | tf_op jit(solution)/shard_map/attention/pallas_call | solution.py:386
  137.7 146.7 %experts.1 = (bf16[128,4096]{1,0:T(8,128)(2,1)}, bf16[8,1024,256]{2,1,0:T(8,128)(2,1)}, bf16[8,256,4096]{2,1,0:T(8,128)(2,1)}) custom-call(bf16[128,4224]{1,0:T(8,128)(2,1)} %get-tuple-element.9.ext, f32[128,4096]{1,0:T(8,128)} %get-tuple-element.10.hs, bf16[2,4096,256]{2,1,0:T(8,128)(2,1)} %up.3, bf16[8,4096,256]{2,1,0:T(8,128)(2,1)} %get-tuple-element.11.early, ...), custom_call_target="tpu_custom_call" | custom-call | tf_op jit(solution)/shard_map/experts/pallas_call | solution.py:635
  284.4 2.3 copy.22
  (2 shorter events, 0.0 us)

commit v4 on v3

--- a/solution.py
+++ b/solution.py
@@ -13,7 +13,7 @@
 ATT_EXP = 4
 EXT = D + 128
 ROWS = 128
-EARLY = 4
+SLOT = {0: 0, 1: 1, 3: 2, 2: 3}
 epsilon = 1e-05
 MESH = pl.DeviceIdType.MESH
 ANY = pl.BlockSpec(memory_space=pl.ANY)
@@ -61,66 +61,76 @@
     )
 
 
-def spread_over_z(at, own, gathered, full, p, sems):
-    s1, r1, s2, r2, s3, r3 = sems
-    n = full // 16
-    spans = (
-        pl.ds(pl.multiple_of(p.c * (4 * n) + p.y * n, n), n),
-        pl.ds(pl.multiple_of(8 * n + p.c * (4 * n) + p.x * n, n), n),
-    )
-    halves = tuple(pl.ds(pl.multiple_of(8 * n * h + p.c * (4 * n), 4 * n), 4 * n) for h in range(2))
+def spread_over_z(at, own, gathered, bands, p, sems):
+    s1, r1, s2, r2, s3, r3, s4, r4 = sems
+
+    def span(h, size):
+        base, n, y_first = bands[h]
+        outer, inner = (p.x, p.y) if y_first else (p.y, p.x)
+        row = base + p.c * 16 * n + (outer * 4 * n if size < 16 else 0) + (inner * n if size < 4 else 0)
+        return pl.ds(pl.multiple_of(row, n), size * n)
 
     def first(d, h):
-        return remote(
-            own.at[spans[h]], gathered.at[p.inner, spans[h]], s1.at[at, d - 1, h], r1.at[at, d - 1, h], p.along_z(d)
-        )
+        piece = span(h, 1)
+        return remote(own.at[piece], gathered.at[p.inner, piece], s1.at[at, d - 1, h], r1.at[at, d - 1, h], p.along_z(d))
 
     def second(d, h, e):
-        j = (p.inner - d + 4) % 4
-        peer = p.along_y(e) if h == 0 else p.along_x(e)
-        block = gathered.at[j, spans[h]]
+        block = gathered.at[(p.inner - d + 4) % 4, span(h, 1)]
+        peer = p.along_y(e) if bands[h][2] else p.along_x(e)
         return remote(block, block, s2.at[at, d - 1, h, e - 1], r2.at[at, d - 1, h, e - 1], peer)
 
-    def third(d, h):
-        j = (p.inner - d + 4) % 4
-        block = gathered.at[j, halves[h]]
-        return remote(block, block, s3.at[at, d - 1, h], r3.at[at, d - 1, h], p.sibling())
+    def third(d, h, e):
+        block = gathered.at[(p.inner - d + 4) % 4, span(h, 4)]
+        peer = p.along_x(e) if bands[h][2] else p.along_y(e)
+        return remote(block, block, s3.at[at, d - 1, h, e - 1], r3.at[at, d - 1, h, e - 1], peer)
+
+    def fourth(d, h):
+        block = gathered.at[(p.inner - d + 4) % 4, span(h, 16)]
+        return remote(block, block, s4.at[at, d - 1, h], r4.at[at, d - 1, h], p.sibling())
 
     order = (1, 3, 2)
-    every = [(d, h) for d in order for h in range(2)]
+    every = [(d, h) for d in order for h in range(len(bands))]
 
     def go1():
         for d, h in every:
             first(d, h).start()
 
-    def go2(d):
-        for h in range(2):
+    def go2():
+        for d, h in every:
             first(d, h).wait_recv()
-            for e in (1, 3, 2):
+            for e in order:
                 second(d, h, e).start()
 
-    def go3(d):
-        for h in range(2):
-            for e in (1, 3, 2):
+    def go3():
+        for d, h in every:
+            for e in order:
                 second(d, h, e).wait_recv()
-            third(d, h).start()
+            for e in order:
+                third(d, h, e).start()
+
+    def go4():
+        for d, h in every:
+            for e in order:
+                third(d, h, e).wait_recv()
+            fourth(d, h).start()
 
     def arrived():
         for d, h in every:
-            third(d, h).wait_recv()
+            fourth(d, h).wait_recv()
 
     def sent():
         for d, h in every:
             first(d, h).wait_send()
-            third(d, h).wait_send()
-            for e in (1, 3, 2):
+            fourth(d, h).wait_send()
+            for e in order:
                 second(d, h, e).wait_send()
-
-    return order, go1, go2, go3, arrived, sent
+                third(d, h, e).wait_send()
+
+    return go1, go2, go3, go4, arrived, sent
 
 
 def spread_sems(n):
-    return [DMA((n, 3, 2)), DMA((n, 3, 2)), DMA((n, 3, 2, 3)), DMA((n, 3, 2, 3)), DMA((n, 3, 2)), DMA((n, 3, 2))]
+    return [DMA((n, 3, 2))] * 2 + [DMA((n, 3, 2, 3))] * 4 + [DMA((n, 3, 2))] * 2
 
 
 def square_peers(p):
@@ -250,10 +260,10 @@
 def attention_kernel(
     tok, gain, mlp_gain, chosen, picked, mlp_router, w_in, router, w_out, up, ext, hs, gup,
     normed, gw, gr, kv, gk, ao,
-    s1, r1, s2, r2, s3, r3, ro_s, ro_r, sz, rz, sx, rx, sc, rc, local, ns, fr, ps, sr, ys, yr,
+    s1, r1, s2, r2, s3, r3, s4, r4, ro_s, ro_r, sz, rz, sx, rx, sc, rc, local, ns, fr, ps, sr, ys, yr,
 ):
     p = Place()
-    steps = [(up, gup, True, 2 * m, 2 * m) for m in range(2 * EARLY)]
+    steps = [(up, gup, True, 2 * m, 2 * m) for m in range(8)]
     w = Weights(p, steps, (ns, fr, ps, sr, ys, yr))
     own = [
         pltpu.make_async_copy(w_in, gw.at[p.inner], local.at[0]),
@@ -263,9 +273,9 @@
     for copy in own:
         copy.start()
     meet(square_peers(p) + [p.beyond(), p.pair()])
-    sems = (s1, r1, s2, r2, s3, r3)
-    order, in1, in2, in3, in_arrived, in_sent = spread_over_z(0, w_in, gw, 1024, p, sems)
-    _, out1, out2, out3, out_arrived, out_sent = spread_over_z(1, w_out, ao, 512, p, sems)
+    sems = (s1, r1, s2, r2, s3, r3, s4, r4)
+    in1, in2, in3, in4, in_arrived, in_sent = spread_over_z(0, w_in, gw, ((0, 16, False), (512, 16, True)), p, sems)
+    out1, out2, out3, out4, out_arrived, out_sent = spread_over_z(1, w_out, ao, ((0, 16, True),), p, sems)
     routers = [remote(router, gr.at[p.inner], ro_s.at[d - 1], ro_r.at[d - 1], p.along_z(d)) for d in (1, 2, 3)]
     zs = [remote(kv, gk.at[p.outer, p.inner], sz.at[d - 1], rz.at[d - 1], p.along_z(d)) for d in (1, 2, 3)]
     xs = [remote(gk.at[p.outer], gk.at[p.outer], sx.at[d - 1], rx.at[d - 1], p.along_x(d)) for d in (1, 2, 3)]
@@ -277,15 +287,15 @@
     in1()
     for copy in routers:
         copy.start()
+    w.begin(0)
     norm_rows(tok, gain, normed)
-    for d in order:
-        in2(d)
-    w.begin(0)
-    for d in order:
-        in3(d)
+    in2()
     w.advance(0)
+    in3()
+    w.advance(1)
+    in4()
+    w.advance(2)
     in_arrived()
-    w.advance(1)
     for copy in routers:
         copy.wait_recv()
     own[0].wait()
@@ -312,22 +322,21 @@
     keep = pltpu.make_async_copy(kv, gk.at[p.outer, p.inner], local.at[3])
     keep.start()
     out1()
-    w.advance(2)
+    w.advance(3)
     keep.wait()
     for copy in zs:
         copy.wait_recv()
     for copy in (xs[0], xs[2], xs[1]):
         copy.start()
     cs[0].start()
-    for d in order:
-        out2(d)
-    w.advance(3)
+    out2()
+    w.advance(4)
+    out3()
     for d in (1, 3, 2):
         xs[d - 1].wait_recv()
         cs[d].start()
-    for d in order:
-        out3(d)
-    w.advance(4)
+    w.advance(5)
+    out4()
     for copy in cs:
         copy.wait_recv()
 
@@ -373,7 +382,7 @@
     high = gates.astype(BF)
     ext[:, D:] = jnp.concatenate([high, (gates - high.astype(F32)).astype(BF)], axis=1)
     w.advance(99)
-    for i in range(2 * EARLY):
+    for i in range(8):
         w.settle(i)
     w.drain()
     in_sent()
@@ -388,7 +397,7 @@
         out_shape=(
             jax.ShapeDtypeStruct((ROWS, EXT), BF),
             jax.ShapeDtypeStruct((ROWS, D), F32),
-            jax.ShapeDtypeStruct((8, EARLY * 1024, 256), BF),
+            jax.ShapeDtypeStruct((8, D, 256), BF),
         ),
         in_specs=[VM] * 6 + [ANY] * 4,
         out_specs=(VM, VM, ANY),
@@ -403,47 +412,42 @@
         + spread_sems(2)
         + [DMA((3,))] * 6
         + [DMA((4,))] * 3
-        + weight_sems(2 * EARLY),
+        + weight_sems(8),
         compiler_params=pltpu.CompilerParams(collective_id=1, has_side_effects=True, vmem_limit_bytes=60 * 2**20),
         name="attention",
     )(*arrays)
 
 
 def moe_kernel(
-    ext, hs, up, early, down, out, late, gdn,
+    ext, hs, up, early, down, out, gdn,
     xall, acc, hid, wbuf, dbuf, part, pairbuf, xbuf,
     ns, fr, ps, sr, ys, yr, ts, tr, us, ur, vs, vr, es, er, qs, qr, local, load,
 ):
     p = Place()
-    steps = [(up, late, True, 2 * m, 2 * m - 4 * EARLY) for m in range(2 * EARLY, 8)]
-    steps += [(down, gdn, False, 2 * m, 2 * m) for m in range(8)]
+    steps = [(down, gdn, False, 2 * m, 2 * m) for m in range(8)]
     w = Weights(p, steps, (ns, fr, ps, sr, ys, yr))
     meet(w.peers() + [p.along_x(1), p.along_x(2), p.along_x(3), p.sibling()])
-    def rows(o, h):
-        return xall.at[o, pl.ds(64 * h, 64), :]
-
-    def block(d):
-        return ((p.x + d) % 4) * 2 + p.c
+    def rows(d, h):
+        return xall.at[SLOT[d], p.c, pl.ds(64 * h, 64), :]
 
     def mine(d, h):
         src = ext.at[pl.ds(64 * h, 64), :]
-        return remote(src, rows(p.outer, h), ts.at[(d - 1) // 2, h], tr.at[(d - 1) // 2, h], p.along_x(d))
+        return remote(src, rows(4 - d, h), ts.at[(d - 1) // 2, h], tr.at[(d - 1) // 2, h], p.along_x(d))
 
     def relay(d):
         h = (d - 1) // 2
-        src = rows(block(4 - d), h)
-        return remote(src, src, us.at[h], ur.at[h], p.along_x(d))
+        return remote(rows(4 - d, h), rows(2, h), us.at[h], ur.at[h], p.along_x(d))
 
     def across(d, h):
-        src = ext.at[pl.ds(64 * h, 64), :] if d == 0 else rows(block(d), h)
-        return remote(src, rows(block(d), h), vs.at[d, h], vr.at[d, h], p.sibling())
+        src = ext.at[pl.ds(64 * h, 64), :] if d == 0 else rows(d, h)
+        return remote(src, rows(d, h), vs.at[d, h], vr.at[d, h], p.sibling())
 
     for h in range(2):
         for d in (1, 3):
             mine(d, h if d == 1 else 1 - h).start()
     for h in range(2):
         across(0, h).start()
-    keep = pltpu.make_async_copy(ext, xall.at[p.outer], local.at[2])
+    keep = pltpu.make_async_copy(ext, xall.at[0, p.c], local.at[2])
     keep.start()
     w.begin(0)
 
@@ -453,10 +457,9 @@
             src = own if d == 0 else gathered.at[two]
             yield pltpu.make_async_copy(src, buffer.at[two], load.at[at, d])
 
-    def load_up(m):
-        held, base = (early, 0) if m < EARLY else (late, EARLY)
-        mine_up = up.at[:, pl.ds(1024 * m, 1024), :]
-        return loads(mine_up, held.at[:, pl.ds(1024 * (m - base), 1024), :], wbuf.at[m % 3], m % 3)
+    def load_up(m, slot):
+        span = pl.ds(1024 * m, 1024)
+        return loads(up.at[:, span, :], early.at[:, span, :], wbuf.at[slot], slot)
 
     def load_down(m):
         span = pl.ds(1024 * m, 1024)
@@ -470,33 +473,22 @@
         for copy in copies:
             copy.wait()
 
-    def run_up(m, groups):
-        for d in groups:
-            there = (p.x + d) % 4
-
-            def one(e, carry):
-                tokens = xall[pl.ds(2 * there, 2), :, pl.ds(1024 * m, 1024)].reshape(256, 1024)
-                rows = pl.ds(pl.multiple_of(256 * there, 256), 256)
-                got = jnp.dot(tokens, wbuf[m % 3, e], preferred_element_type=F32)
-                if m == 0:
-                    acc[e, rows, :] = got
-                else:
-                    acc[e, rows, :] += got
-                return carry
-
-            lax.fori_loop(0, 8, one, 0)
-
-    def run_up_all(m):
+    def run_up(m, slot, low, high, first):
         def one(e, carry):
-            tokens = xall[:, :, pl.ds(1024 * m, 1024)].reshape(1024, 1024)
-            acc[e] += jnp.dot(tokens, wbuf[m % 3, e], preferred_element_type=F32)
+            tokens = xall[low:high, :, :, pl.ds(1024 * m, 1024)].reshape((high - low) * 256, 1024)
+            span = slice(256 * low, 256 * high)
+            got = jnp.dot(tokens, wbuf[slot, e], preferred_element_type=F32)
+            if first:
+                acc[e, span, :] = got
+            else:
+                acc[e, span, :] += got
             return carry
 
         lax.fori_loop(0, 8, one, 0)
 
     def gate():
         names = lax.broadcasted_iota(jnp.int32, (128, 256), 0) % 64
-        shares = xall[:, :, D:].reshape(1024, 128)
+        shares = xall[:, :, :, D:].reshape(1024, 128)
 
         def one(e, carry):
             pick = jnp.where(names == p.outer * 8 + e, 1.0, 0.0).astype(BF)
@@ -520,20 +512,18 @@
         return remote(part.at[m, :, 1 - p.c], pairbuf.at[m], es.at[m], er.at[m], p.sibling())
 
     def give(m, d):
-        there = (p.x + d) % 4
-        return remote(part.at[m, there, p.c], xbuf.at[m, d - 1], qs.at[m, d - 1], qr.at[m, d - 1], p.along_x(d))
+        return remote(part.at[m, SLOT[d], p.c], xbuf.at[m, d - 1], qs.at[m, d - 1], qr.at[m, d - 1], p.along_x(d))
 
     def add_pair(m):
         swap(m).wait_recv()
         for d in (1, 3, 2):
-            there = (p.x + d) % 4
-            total = part[m, there, p.c].astype(F32) + pairbuf[m, there].astype(F32)
-            part[m, there, p.c] = total.astype(BF)
+            total = part[m, SLOT[d], p.c].astype(F32) + pairbuf[m, SLOT[d]].astype(F32)
+            part[m, SLOT[d], p.c] = total.astype(BF)
             give(m, d).start()
 
     def finish(m):
         span = pl.ds(1024 * m, 1024)
-        total = hs[:, span] + part[m, p.x, p.c].astype(F32) + pairbuf[m, p.x].astype(F32)
+        total = hs[:, span] + part[m, 0, p.c].astype(F32) + pairbuf[m, 0].astype(F32)
         for d in (1, 3, 2):
             give(m, d).wait_recv()
             total += xbuf[m, d - 1].astype(F32)
@@ -552,46 +542,49 @@
         across(1, 1).start()
         keep.wait()
         from_sibling(0)
-        for m in range(2):
-            land(load_up(m))
-            run_up(m, (0,))
+        for m in range(3):
+            land(load_up(m, m))
 
     def part_1():
+        w.advance(3)
         mine(1, 1).wait_recv()
         across(3, 1).start()
         mine(3, 0).wait_recv()
         across(1, 0).start()
         from_sibling(1)
         from_sibling(3)
-        for m in range(2):
-            run_up(m, (1, 3))
+        run_up(0, 0, 0, 3, True)
+        fetch(load_up(3, 0))
+        run_up(1, 1, 0, 3, False)
+        w.advance(4)
+        run_up(2, 2, 0, 3, False)
 
     def part_2():
         for d in (1, 3):
             relay(d).wait_recv()
             across(2, (d - 1) // 2).start()
-        if EARLY > 2:
-            fetch(load_up(2))
+        land(load_up(3, 0))
+        run_up(3, 0, 0, 3, False)
+        w.advance(5)
         from_sibling(2)
-        for m in range(2):
-            run_up(m, (2,))
-        if EARLY > 3:
-            fetch(load_up(3))
-
-    def rest_up(m):
-        if m >= EARLY:
-            w.settle(2 * (m - EARLY))
-            w.settle(2 * (m - EARLY) + 1)
-            fetch(load_up(m))
-        land(load_up(m))
-        run_up_all(m)
-        if m == 3:
-            gate()
+        run_up(1, 1, 3, 4, True)
+        fetch(load_up(0, 1))
+        run_up(2, 2, 3, 4, False)
+        w.advance(6)
+        run_up(3, 0, 3, 4, False)
+        load_soon(0)
+        land(load_up(0, 1))
+        run_up(0, 1, 3, 4, False)
+        gate()
+
+    def load_soon(m):
+        w.settle(2 * m)
+        w.settle(2 * m + 1)
+        fetch(load_down(m))
 
     def produce(m):
-        w.settle(2 * (4 - EARLY + m))
-        w.settle(2 * (4 - EARLY + m) + 1)
-        fetch(load_down(m))
+        if m > 1:
+            load_soon(m)
         if m > 0:
             add_pair(m - 1)
         if m > 1:
@@ -600,20 +593,21 @@
         run_down(m)
         swap(m).start()
 
-    fetch(load_up(0))
-    fetch(load_up(1))
+    for m in range(3):
+        fetch(load_up(m, m))
     w.advance(0)
     part_0()
     w.advance(2)
     part_1()
-    w.advance(3)
     part_2()
-    for m in (2, 3):
-        w.advance(2 * (m - EARLY) + 4 if m >= EARLY else 0)
-        rest_up(m)
-    for m in range(4):
-        w.advance(2 * (4 - EARLY + m) + 4)
-        produce(m)
+    w.advance(7)
+    load_soon(1)
+    produce(0)
+    w.advance(8)
+    produce(1)
+    w.advance(10)
+    produce(2)
+    produce(3)
     add_pair(3)
     finish(2)
     finish(3)
@@ -636,13 +630,12 @@
         moe_kernel,
         out_shape=(
             jax.ShapeDtypeStruct((ROWS, D), BF),
-            jax.ShapeDtypeStruct((8, max(1, 4 - EARLY) * 1024, 256), BF),
             jax.ShapeDtypeStruct((8, 256, D), BF),
         ),
         in_specs=[ANY, VM, ANY, ANY, ANY],
-        out_specs=(VM, ANY, ANY),
+        out_specs=(VM, ANY),
         scratch_shapes=[
-            pltpu.VMEM((8, ROWS, EXT), BF),
+            pltpu.VMEM((4, 2, ROWS, EXT), BF),
             pltpu.VMEM((8, 1024, 256), F32),
             pltpu.VMEM((1024, 2048), BF),
             pltpu.VMEM((3, 8, 1024, 256), BF),
@@ -651,7 +644,7 @@
             pltpu.VMEM((4, 4, ROWS, 1024), BF),
             pltpu.VMEM((4, 3, ROWS, 1024), BF),
         ]
-        + weight_sems(16 - 2 * EARLY)
+        + weight_sems(8)
         + [
             DMA((2, 2)), DMA((2, 2)), DMA((2,)), DMA((2,)), DMA((4, 2)), DMA((4, 2)),
             DMA((4,)), DMA((4,)), DMA((4, 3)), DMA((4, 3)), DMA((3,)), DMA((5, 4)),

time: 287 us -> 269 us (0.937)
  Pallas kernels: 282 us -> 263 us
    pallas_call x1, Pallas kernels: 135 us -> 120 us  [attention(): pl.pallas_call(attention_kernel, out_shape=(jax.ShapeDtypeStruct((ROWS, E...]
    pallas_call x1, Pallas kernels: 147 us -> 143 us  [moe(): pl.pallas_call(moe_kernel, out_shape=(jax.ShapeDtypeStruct((ROWS, D), BF)...]
where the time goes in v4:
time: 269 us; the launch traced here: 268 us
  Pallas kernels  263 us (98%)
  local copies, waits for them, and re-layouts  3.73 us (1%)
    pallas_call x1, Pallas kernels, moe(): pl.pallas_call(moe_kernel, out_shape=(jax.ShapeDtypeStruct((ROWS, D), BF)...  143 us
    pallas_call x1, Pallas kernels, attention(): pl.pallas_call(attention_kernel, out_shape=(jax.ShapeDtypeStruct((ROWS, E...  120 us

profile of v4, /device:TPU:1, one launch (start us, length us, event | category | flops | bytes accessed | tf_op | source)
XLA Modules:
  0.0 268.3 jit_solution(17850701194366237532)
XLA Ops:
  0.0 0.7 fusion.1
  0.7 0.7 fusion
  1.5 0.7 copy.20.picked
  2.2 0.7 copy.19.chosen
  2.9 120.1 %attention.1 = (bf16[128,4224]{1,0:T(8,128)(2,1)}, f32[128,4096]{1,0:T(8,128)}, bf16[8,4096,256]{2,1,0:T(8,128)(2,1)}) custom-call(bf16[128,4096]{1,0:T(8,128)(2,1)} %tok.1, f32[1,4096]{1,0:T(1,128)} %bitcast.6, f32[1,4096]{1,0:T(1,128)} %bitcast.7, f32[128,8]{1,0:T(8,128)} %copy.19.chosen, f32[128,64]{1,0:T(8,128)} %copy.20.picked, ...), custom_call_target="tpu_custom_call" | custom-call | tf_op jit(solution)/shard_map/attention/pallas_call | solution.py:395
  123.0 143.0 %experts.1 = (bf16[128,4096]{1,0:T(8,128)(2,1)}, bf16[8,256,4096]{2,1,0:T(8,128)(2,1)}) custom-call(bf16[128,4224]{1,0:T(8,128)(2,1)} %get-tuple-element.9.ext, f32[128,4096]{1,0:T(8,128)} %get-tuple-element.10.hs, bf16[2,4096,256]{2,1,0:T(8,128)(2,1)} %up.3, bf16[8,4096,256]{2,1,0:T(8,128)(2,1)} %get-tuple-element.11.early, bf16[2,256,4096]{2,1,0:T(8,128)(2,1)} %down.1), custom_call_target="tpu_custom_call" | custom-call | tf_op jit(solution)/shard_map/experts/pallas_call | solution.py:629
  266.0 2.3 copy.22
  (2 shorter events, 0.0 us)

commit v5 on v4

--- a/solution.py
+++ b/solution.py
@@ -498,7 +498,7 @@
 
         lax.fori_loop(0, 8, one, 0)
 
-    def run_down(m):
+    def run_down(m, h):
         def one(n, carry):
             span = pl.ds(pl.multiple_of(256 * n, 256), 256)
             weights = dbuf[m % 2, :, :, span].reshape(2048, 256)
@@ -506,26 +506,35 @@
             part[m, :, :, :, span] = got.astype(BF).reshape(4, 2, 128, 256)
             return carry
 
-        lax.fori_loop(0, 4, one, 0)
-
-    def swap(m):
-        return remote(part.at[m, :, 1 - p.c], pairbuf.at[m], es.at[m], er.at[m], p.sibling())
-
-    def give(m, d):
-        return remote(part.at[m, SLOT[d], p.c], xbuf.at[m, d - 1], qs.at[m, d - 1], qr.at[m, d - 1], p.along_x(d))
+        lax.fori_loop(2 * h, 2 * h + 2, one, 0)
+
+    def half(h):
+        return pl.ds(512 * h, 512)
+
+    def swap(m, h):
+        src = part.at[m, :, 1 - p.c, :, half(h)]
+        return remote(src, pairbuf.at[m, :, :, half(h)], es.at[m, h], er.at[m, h], p.sibling())
+
+    def give(m, h, d):
+        src = part.at[m, SLOT[d], p.c, :, half(h)]
+        dst = xbuf.at[m, d - 1, :, half(h)]
+        return remote(src, dst, qs.at[m, h, d - 1], qr.at[m, h, d - 1], p.along_x(d))
 
     def add_pair(m):
-        swap(m).wait_recv()
-        for d in (1, 3, 2):
-            total = part[m, SLOT[d], p.c].astype(F32) + pairbuf[m, SLOT[d]].astype(F32)
-            part[m, SLOT[d], p.c] = total.astype(BF)
-            give(m, d).start()
+        for h in range(2):
+            swap(m, h).wait_recv()
+            cols = slice(512 * h, 512 * (h + 1))
+            for d in (2, 1, 3):
+                total = part[m, SLOT[d], p.c, :, cols].astype(F32) + pairbuf[m, SLOT[d], :, cols].astype(F32)
+                part[m, SLOT[d], p.c, :, cols] = total.astype(BF)
+                give(m, h, d).start()
 
     def finish(m):
         span = pl.ds(1024 * m, 1024)
         total = hs[:, span] + part[m, 0, p.c].astype(F32) + pairbuf[m, 0].astype(F32)
         for d in (1, 3, 2):
-            give(m, d).wait_recv()
+            for h in range(2):
+                give(m, h, d).wait_recv()
             total += xbuf[m, d - 1].astype(F32)
         out[:, span] = total.astype(BF)
 
@@ -590,8 +599,9 @@
         if m > 1:
             finish(m - 2)
         land(load_down(m))
-        run_down(m)
-        swap(m).start()
+        for h in range(2):
+            run_down(m, h)
+            swap(m, h).start()
 
     for m in range(3):
         fetch(load_up(m, m))
@@ -620,9 +630,10 @@
     for d in (1, 3):
         relay(d).wait_send()
     for m in range(4):
-        swap(m).wait_send()
-        for d in (1, 2, 3):
-            give(m, d).wait_send()
+        for h in range(2):
+            swap(m, h).wait_send()
+            for d in (1, 2, 3):
+                give(m, h, d).wait_send()
 
 
 def moe(ext, hidden_state, w_up, gathered_up, w_down):
@@ -647,7 +658,7 @@
         + weight_sems(8)
         + [
             DMA((2, 2)), DMA((2, 2)), DMA((2,)), DMA((2,)), DMA((4, 2)), DMA((4, 2)),
-            DMA((4,)), DMA((4,)), DMA((4, 3)), DMA((4, 3)), DMA((3,)), DMA((5, 4)),
+            DMA((4, 2)), DMA((4, 2)), DMA((4, 2, 3)), DMA((4, 2, 3)), DMA((3,)), DMA((5, 4)),
         ],
         compiler_params=pltpu.CompilerParams(collective_id=3, has_side_effects=True, vmem_limit_bytes=60 * 2**20),
         name="experts",

time: 269 us -> 267 us (level)
  no operation moved by 1% of the time
where the time goes in v5:
time: 267 us
  Pallas kernels  261 us (98%)
  local copies, waits for them, and re-layouts  3.73 us (1%)
    pallas_call x1, Pallas kernels, moe(): pl.pallas_call(moe_kernel, out_shape=(jax.ShapeDtypeStruct((ROWS, D), BF)...  141 us
    pallas_call x1, Pallas kernels, attention(): pl.pallas_call(attention_kernel, out_shape=(jax.ShapeDtypeStruct((ROWS, E...  120 us

profile of v5, /device:TPU:1, one launch (start us, length us, event | category | flops | bytes accessed | tf_op | source)
XLA Modules:
  0.0 266.5 jit_solution(13965631272543931617)
XLA Ops:
  0.0 0.7 fusion.1
  0.7 0.7 fusion
  1.5 0.7 copy.20.picked
  2.2 0.7 copy.19.chosen
  2.9 120.1 %attention.1 = (bf16[128,4224]{1,0:T(8,128)(2,1)}, f32[128,4096]{1,0:T(8,128)}, bf16[8,4096,256]{2,1,0:T(8,128)(2,1)}) custom-call(bf16[128,4096]{1,0:T(8,128)(2,1)} %tok.1, f32[1,4096]{1,0:T(1,128)} %bitcast.6, f32[1,4096]{1,0:T(1,128)} %bitcast.7, f32[128,8]{1,0:T(8,128)} %copy.19.chosen, f32[128,64]{1,0:T(8,128)} %copy.20.picked, ...), custom_call_target="tpu_custom_call" | custom-call | tf_op jit(solution)/shard_map/attention/pallas_call | solution.py:395
  123.0 141.3 %experts.1 = (bf16[128,4096]{1,0:T(8,128)(2,1)}, bf16[8,256,4096]{2,1,0:T(8,128)(2,1)}) custom-call(bf16[128,4224]{1,0:T(8,128)(2,1)} %get-tuple-element.9.ext, f32[128,4096]{1,0:T(8,128)} %get-tuple-element.10.hs, bf16[2,4096,256]{2,1,0:T(8,128)(2,1)} %up.3, bf16[8,4096,256]{2,1,0:T(8,128)(2,1)} %get-tuple-element.11.early, bf16[2,256,4096]{2,1,0:T(8,128)(2,1)} %down.1), custom_call_target="tpu_custom_call" | custom-call | tf_op jit(solution)/shard_map/experts/pallas_call | solution.py:640
  264.2 2.3 copy.22
  (2 shorter events, 0.0 us)
